TPU v7x, 32 devices: a whole 2x2x4 slice. The times are simulated.
32 devices in a mesh: dp: 16 (over z, y, core), tensor: 2 (over x).
Axes of the slice: x: 2, y: 2, z: 4, core: 2. Of those that a mesh axis runs over, the one named last changes fastest.
Arguments:
- tokens: bfloat16 [32768, 768], P(('dp', 'tensor')), may hold values from -6 to 6
- memory: bfloat16 [16, 1500, 768], P('dp'), may hold values from -6 to 6
- seg_ids: int32 [32768], P(('dp', 'tensor')), may hold values from 0 to 4, as said below
- positions: int32 [32768], P(('dp', 'tensor')), may hold values from 0 to 1535, as said below
- grad_output: bfloat16 [32768, 768], P(('dp', 'tensor')), may hold values from -6 to 6
- attn_in: bfloat16 [768, 3, 768], P('dp', None, 'tensor'), may hold values from -0.21875 to 0.21875
- attn_out: bfloat16 [768, 768], P('tensor', 'dp'), may hold values from -2.5 to 2.5
- cross_q: bfloat16 [768, 768], P('dp', 'tensor'), may hold values from -0.21875 to 0.21875
- cross_kv: bfloat16 [768, 2, 768], P('dp', None, 'tensor'), may hold values from -0.21875 to 0.21875
- cross_out: bfloat16 [768, 768], P('tensor', 'dp'), may hold values from -2.5 to 2.5
- mlp_in: bfloat16 [768, 3072], P('dp', 'tensor'), may hold values from -0.21875 to 0.21875
- mlp_out: bfloat16 [3072, 768], P('tensor', 'dp'), may hold values from -0.109375 to 0.109375
- norm_gain: float32 [3, 768], replicated, may hold values from 0.5 to 1.5
- norm_bias: float32 [3, 768], replicated, may hold values from -1 to 1
- proj_bias: float32 [6, 768], replicated, may hold values from -0.5 to 0.5
- mlp_bias: float32 [3072], replicated, may hold values from -1 to 1
- out_bias: float32 [768], replicated, may hold values from -2.5 to 2.5
Outputs:
- output: bfloat16 [32768, 768], P(('dp', 'tensor'))
- grad_tokens: float32 [32768, 768], P(('dp', 'tensor'))
- grad_attn_in: float32 [768, 3, 768], P('dp', None, 'tensor')
- grad_attn_out: float32 [768, 768], P('tensor', 'dp')
- grad_cross_q: float32 [768, 768], P('dp', 'tensor')
- grad_cross_kv: float32 [768, 2, 768], P('dp', None, 'tensor')
- grad_cross_out: float32 [768, 768], P('tensor', 'dp')
- grad_mlp_in: float32 [768, 3072], P('dp', 'tensor')
- grad_mlp_out: float32 [3072, 768], P('tensor', 'dp')
- grad_norm_gain: float32 [3, 768], replicated
- grad_norm_bias: float32 [3, 768], replicated
- grad_proj_bias: float32 [6, 768], replicated
- grad_mlp_bias: float32 [3072], replicated
- grad_out_bias: float32 [768], replicated
Inputs may be any that keep to these rules, and one draw needn't show every extreme that they name: `seg_ids`: within each group of 2048 consecutive tokens, the first 1024 are 0 (the prompt); the rest are 4 runs numbered 1 to 4 in order, each of 1 to 512 tokens, one of exactly 512 tokens. Prompt tokens have positions 0, 1, ... in order; each continuation's tokens have positions 1024, 1025, ... in order.
All inputs are finite; a program needn't handle non-finite values.
Results may differ from a plain program's by a relative error of at most 0.029.
Values may be sent and summed in bfloat16 or wider, within the bound.
A program may use at most 256 MiB of HBM per device.

v0:
```python
import functools, jax, jax.numpy as jnp
from jax import lax
from jax.experimental import pallas as pl
from jax.experimental.pallas import tpu as pltpu
from jax.sharding import Mesh
from jax.sharding import PartitionSpec as P
BLK=256
HEAD=64
LANES=128
NEG=-1e30
LOG2E=1.4426950408889634
F32=jnp.float32; BF=jnp.bfloat16

def lane_ids(rows): return lax.broadcasted_iota(jnp.int32,(rows,LANES),1)

def nt(a,b): return lax.dot_general(a,b,(((1,),(1,)),((),())),preferred_element_type=F32)
def nn(a,b): return lax.dot_general(a,b,(((1,),(0,)),((),())),preferred_element_type=F32)
def tn(a,b): return lax.dot_general(a,b,(((0,),(0,)),((),())),preferred_element_type=F32)

def pick(head, lanes): return (lanes<64) if head==0 else (lanes>=64)

def places(core, half):
    return (core * half, (1 - core) * half)


def rows_at(base, offset, count):
    return pl.ds(pl.multiple_of(base + offset, BLK), count)


def self_fwd_kernel(core_ref,kept_ref,come_ref,segq_ref,segk_ref,own_ref,sent_ref,lse_ref,q_ref,k_ref,vx_ref,o_ref):
    half=kept_ref.shape[1]; rows=2*half; n=rows//BLK
    core=core_ref[0]
    for ref,base in zip((kept_ref,come_ref),places(core,half)):
        at=rows_at(base,0,half)
        q_ref[at,:]=ref[0]
        k_ref[at,:]=ref[1]
        vx_ref[at,:LANES]=ref[2]
    vx_ref[:,LANES:]=jnp.ones((rows,LANES),BF)
    lanes=lane_ids(BLK)
    for i in range(n):
        r0=i*BLK; kn=r0+BLK
        q=q_ref[r0:kn,:]
        outs=[];lses=[]
        for h in range(2):
            qm=jnp.where(pick(h,lanes),q,jnp.zeros_like(q))
            s=nt(qm,k_ref[:kn,:])
            cut = half if i>=n//2 else r0
            a=s[:,:cut] if cut>0 else None
            b=s[:,cut:]
            w=kn-cut
            qi=lax.broadcasted_iota(jnp.int32,(BLK,w),0)+(r0-cut)
            kj=lax.broadcasted_iota(jnp.int32,(BLK,w),1)
            ok=kj<=qi
            if i>=n//2:
                ok=ok&(segk_ref[:,:kn-half]==segq_ref[r0-half:kn-half,:])
            b=jnp.where(ok,b,NEG)
            m=jnp.max(b,-1,keepdims=True)
            if a is not None: m=jnp.maximum(m,jnp.max(a,-1,keepdims=True))
            pb=jnp.exp2(b-m).astype(BF)
            ox=nn(pb,vx_ref[cut:kn,:])
            if a is not None:
                pa=jnp.exp2(a-m).astype(BF)
                ox=ox+nn(pa,vx_ref[:cut,:])
            l=ox[:,LANES:]
            outs.append(ox[:,:LANES]/l); lses.append(m+jnp.log2(l))
        sel=lanes<64
        o_ref[r0:kn,:]=jnp.where(sel,outs[0],outs[1]).astype(BF)
        lse_ref[r0:kn,:]=jnp.where(sel,lses[0],lses[1])
    for ref,base in zip((own_ref,sent_ref),places(core,half)):
        ref[...]=o_ref[rows_at(base,0,half),:]


def scalar():
    return pl.BlockSpec(memory_space=pltpu.SMEM)


def pair_cost(pairs,passes,nbytes):
    return pl.CostEstimate(flops=int(pairs*passes*64),bytes_accessed=int(nbytes)//8,transcendentals=int(pairs)//8)


def self_fwd(core,kept,come,segq,segk):
    half,part=kept.shape[1:]; rows=2*half
    three=pl.BlockSpec((3,half,LANES),lambda p:(0,0,p))
    one=pl.BlockSpec((half,LANES),lambda p:(0,p))
    n=rows//BLK
    return pl.pallas_call(self_fwd_kernel,
        grid=(part//LANES,),
        in_specs=[scalar(),three,three,pl.BlockSpec(segq.shape,lambda p:(0,0)),pl.BlockSpec(segk.shape,lambda p:(0,0))],
        out_specs=[one,one,pl.BlockSpec((rows,LANES),lambda p:(0,p))],
        out_shape=[jax.ShapeDtypeStruct((half,part),BF),jax.ShapeDtypeStruct((half,part),BF),jax.ShapeDtypeStruct((rows,part),F32)],
        scratch_shapes=[pltpu.VMEM((rows,LANES),BF),pltpu.VMEM((rows,LANES),BF),pltpu.VMEM((rows,2*LANES),BF),pltpu.VMEM((rows,LANES),BF)],
        compiler_params=pltpu.CompilerParams(vmem_limit_bytes=60*2**20),
        cost_estimate=pair_cost(n*(n+1)//2*BLK*BLK*(part//HEAD),2,12*rows*part),
        name="self_fwd",
    )(core,kept,come,segq,segk)

def cross_fwd_kernel(frames,q_ref,k_ref,v_ref,o_ref,lse_ref,kx_ref,vx_ref):
    rows=q_ref.shape[0]; n=rows//BLK; kp=k_ref.shape[0]
    tail=frames//BLK*BLK
    kx_ref[...]=k_ref[...]
    vx_ref[:,:LANES]=v_ref[...]
    vx_ref[:,LANES:]=jnp.ones((kp,LANES),BF)
    if frames<kp:
        keep=lax.broadcasted_iota(jnp.int32,(kp-tail,LANES),0)+tail<frames
        kx_ref[tail:,:]=jnp.where(keep,k_ref[tail:,:],jnp.zeros((),BF))
        vx_ref[tail:,:LANES]=jnp.where(keep,v_ref[tail:,:],jnp.zeros((),BF))
    lanes=lane_ids(BLK)
    for i in range(n):
        r0=i*BLK
        q=q_ref[r0:r0+BLK,:]
        outs=[];lses=[]
        for h in range(2):
            qm=jnp.where(pick(h,lanes),q,jnp.zeros_like(q))
            s=nt(qm,kx_ref[...])
            if frames<kp:
                kj=lax.broadcasted_iota(jnp.int32,(BLK,kp-tail),1)+tail
                s=jnp.concatenate([s[:,:tail],jnp.where(kj<frames,s[:,tail:],NEG)],axis=1)
            m=jnp.max(s,-1,keepdims=True)
            p=jnp.exp2(s-m).astype(BF)
            ox=nn(p,vx_ref[...])
            l=ox[:,LANES:]
            outs.append(ox[:,:LANES]/l); lses.append(m+jnp.log2(l))
        sel=lanes<64
        o_ref[r0:r0+BLK,:]=jnp.where(sel,outs[0],outs[1]).astype(BF)
        lse_ref[r0:r0+BLK,:]=jnp.where(sel,lses[0],lses[1])

def cross_fwd(q,kv,frames,heads):
    rows=q.shape[0]; npair=heads//2; kp=kv.shape[0]
    return pl.pallas_call(functools.partial(cross_fwd_kernel,frames),
        grid=(npair,),
        in_specs=[pl.BlockSpec((rows,LANES),lambda p:(0,p)),
                  pl.BlockSpec((kp,LANES),lambda p:(0,p)),
                  pl.BlockSpec((kp,LANES),lambda p:(0,npair+p))],
        out_specs=[pl.BlockSpec((rows,LANES),lambda p:(0,p)),pl.BlockSpec((rows,LANES),lambda p:(0,p))],
        out_shape=[jax.ShapeDtypeStruct((rows,heads*64),BF),jax.ShapeDtypeStruct((rows,heads*64),F32)],
        scratch_shapes=[pltpu.VMEM((kp,LANES),BF),pltpu.VMEM((kp,2*LANES),BF)],
        compiler_params=pltpu.CompilerParams(vmem_limit_bytes=60*2**20),
        cost_estimate=pair_cost(rows*kp*heads,2,8*rows*heads*64+4*kp*heads*64),
        name="cross_fwd",
    )(q,kv,kv)

def split3(x):
    hi=x.astype(BF); r=x-hi.astype(F32); mid=r.astype(BF); lo=(r-mid.astype(F32)).astype(BF)
    return hi,mid,lo

def aug(value,head,lanes,one_lane):
    hi,mid,lo=split3(-value)
    z=jnp.zeros(lanes.shape,F32)
    b=64*head
    x=jnp.where(lanes==b,hi.astype(F32),jnp.where(lanes==b+1,mid.astype(F32),jnp.where(lanes==b+2,lo.astype(F32),z)))
    if one_lane: x=jnp.where(lanes==b+3,1.0,x)
    return x.astype(BF)

def build_q(q,do,o,lse,at,qx_ref,dox_ref,masked):
    lanes=lane_ids(BLK)
    prod=do.astype(F32)*o.astype(F32)
    for h in range(2):
        sel=pick(h,lanes)
        delta=jnp.sum(jnp.where(sel,prod,0.0),-1,keepdims=True)
        qx_ref[h,at,:LANES]=jnp.where(sel,q,jnp.zeros((),BF))
        qx_ref[h,at,LANES:]=aug(lse,h,lanes,masked)
        dox_ref[h,at,:LANES]=jnp.where(sel,do,jnp.zeros((),BF))
        dox_ref[h,at,LANES:]=aug(delta,h,lanes,False)

def build_k(k,v,r0,at,kx_ref,km_ref,vx_ref,frames):
    lanes=lane_ids(BLK)
    low=lanes%64
    ones=jnp.where(low<3,1.0,0.0)
    kones=ones
    if frames is not None and r0+BLK>frames:
        bad=lax.broadcasted_iota(jnp.int32,(BLK,LANES),0)+r0>=frames
        k=jnp.where(bad,jnp.zeros((),BF),k); v=jnp.where(bad,jnp.zeros((),BF),v)
        kones=jnp.where(bad&(low==3),NEG,ones)
    kx_ref[at,:LANES]=k; kx_ref[at,LANES:]=kones.astype(BF)
    vx_ref[at,:LANES]=v; vx_ref[at,LANES:]=ones.astype(BF)
    for h in range(2): km_ref[h,at,:]=jnp.where(pick(h,lanes),k,jnp.zeros((),BF))

def block_back(kx,vx,km,qx,dox,mask):
    s=nt(kx,qx)
    if mask is not None:
        cut=s.shape[0]-mask.shape[0]
        low=jnp.where(mask,s[cut:],NEG)
        s=jnp.concatenate([s[:cut],low],0) if cut else low
    p=jnp.exp2(s)
    dp=nt(vx,dox)
    ds=(p*dp).astype(BF)
    pb=p.astype(BF)
    dv=nn(pb,dox[:,:LANES])
    dk=nn(ds,qx[:,:LANES])
    dq=tn(ds,km)
    return dv,dk,dq

def self_bwd_kernel(core_ref,kept_ref,come_ref,do_ref,do_come_ref,o_ref,o_sent_ref,lse_ref,segq_ref,segk_ref,own_ref,sent_ref,
                    qx_ref,dox_ref,kx_ref,km_ref,vx_ref,dqa_ref,dka_ref,dva_ref):
    half=kept_ref.shape[1]; rows=2*half; n=rows//BLK
    core=core_ref[0]
    for ref,d,o,base in zip((kept_ref,come_ref),(do_ref,do_come_ref),(o_ref,o_sent_ref),places(core,half)):
        for r0 in range(0,half,BLK):
            here=slice(r0,r0+BLK); at=rows_at(base,r0,BLK)
            build_q(ref[0,here,:],d[here,:],o[here,:],lse_ref[at,:],at,qx_ref,dox_ref,False)
            build_k(ref[1,here,:],ref[2,here,:],0,at,kx_ref,km_ref,vx_ref,None)
    dka_ref[...]=jnp.zeros_like(dka_ref)
    dva_ref[...]=jnp.zeros_like(dva_ref)
    for i in range(n):
        r0=i*BLK; kn=r0+BLK; at=slice(r0,kn)
        cut=half if i>=n//2 else r0
        w=kn-cut
        mask=lax.broadcasted_iota(jnp.int32,(w,BLK),0)<=lax.broadcasted_iota(jnp.int32,(w,BLK),1)+(r0-cut)
        if i>=n//2: mask=mask&(segk_ref[:kn-half,:]==segq_ref[i-n//2])
        r=[block_back(kx_ref[:kn,:],vx_ref[:kn,:],km_ref[h,:kn,:],qx_ref[h,at,:],dox_ref[h,at,:],mask) for h in range(2)]
        dva_ref[:kn,:]+=r[0][0]+r[1][0]
        dka_ref[:kn,:]+=r[0][1]+r[1][1]
        dqa_ref[at,:]=((r[0][2]+r[1][2])*0.125).astype(BF)
    for ref,base in zip((own_ref,sent_ref),places(core,half)):
        at=rows_at(base,0,half)
        ref[0]=dqa_ref[at,:]
        ref[1]=(dka_ref[at,:]*(1/LOG2E)).astype(BF)
        ref[2]=dva_ref[at,:].astype(BF)

def self_bwd(core,kept,come,do,do_come,o,o_sent,lse,segq,segk):
    half,part=kept.shape[1:]; rows=2*half
    three=pl.BlockSpec((3,half,LANES),lambda p:(0,0,p))
    one=pl.BlockSpec((half,LANES),lambda p:(0,p))
    out=jax.ShapeDtypeStruct((3,half,part),BF)
    n=rows//BLK
    return pl.pallas_call(self_bwd_kernel,
        grid=(part//LANES,),
        in_specs=[scalar(),three,three,one,one,one,one,pl.BlockSpec((rows,LANES),lambda p:(0,p)),
                  pl.BlockSpec(segq.shape,lambda p:(0,0,0)),pl.BlockSpec(segk.shape,lambda p:(0,0))],
        out_specs=[three,three],
        out_shape=[out,out],
        scratch_shapes=[pltpu.VMEM((2,rows,2*LANES),BF),pltpu.VMEM((2,rows,2*LANES),BF),pltpu.VMEM((rows,2*LANES),BF),
                        pltpu.VMEM((2,rows,LANES),BF),pltpu.VMEM((rows,2*LANES),BF),pltpu.VMEM((rows,LANES),BF),
                        pltpu.VMEM((rows,LANES),F32),pltpu.VMEM((rows,LANES),F32)],
        compiler_params=pltpu.CompilerParams(vmem_limit_bytes=60*2**20),
        cost_estimate=pair_cost(n*(n+1)//2*BLK*BLK*(part//HEAD),5,20*rows*part),
        name="self_bwd",
    )(core,kept,come,do,do_come,o,o_sent,lse,segq,segk)

def cross_bwd_kernel(frames,q_ref,k_ref,v_ref,do_ref,o_ref,lse_ref,dq_ref,dk_ref,dv_ref,
                     qx_ref,dox_ref,kx_ref,km_ref,vx_ref,dka_ref,dva_ref):
    rows=q_ref.shape[0]; n=rows//BLK; kp=k_ref.shape[0]; nk=kp//BLK
    for r0 in range(0,rows,BLK):
        at=slice(r0,r0+BLK)
        build_q(q_ref[at,:],do_ref[at,:],o_ref[at,:],lse_ref[at,:],at,qx_ref,dox_ref,True)
    for r0 in range(0,kp,BLK):
        at=slice(r0,r0+BLK)
        build_k(k_ref[at,:],v_ref[at,:],r0,at,kx_ref,km_ref,vx_ref,frames)
    for i in range(rows//BLK):
        at=slice(i*BLK,(i+1)*BLK)
        r=[block_back(kx_ref[...],vx_ref[...],km_ref[h],qx_ref[h,at,:],dox_ref[h,at,:],None) for h in range(2)]
        dv=r[0][0]+r[1][0]; dk=r[0][1]+r[1][1]
        if i==0: dva_ref[...]=dv; dka_ref[...]=dk
        else: dva_ref[...]+=dv; dka_ref[...]+=dk
        dq_ref[at,:]=((r[0][2]+r[1][2])*0.125).astype(BF)
    dk_ref[...]=(dka_ref[...]*(1/LOG2E)).astype(BF)
    dv_ref[...]=dva_ref[...].astype(BF)

def cross_bwd(q,kv,frames,do,o,lse,heads):
    rows=q.shape[0]; npair=heads//2; kp=kv.shape[0]
    big=lambda f:pl.BlockSpec((rows,LANES),f)
    kb=lambda f:pl.BlockSpec((kp,LANES),f)
    return pl.pallas_call(functools.partial(cross_bwd_kernel,frames),
        grid=(npair,),
        in_specs=[big(lambda p:(0,p)),kb(lambda p:(0,p)),kb(lambda p:(0,npair+p)),big(lambda p:(0,p)),big(lambda p:(0,p)),big(lambda p:(0,p))],
        out_specs=[big(lambda p:(0,p)),kb(lambda p:(0,p)),kb(lambda p:(0,p))],
        out_shape=[jax.ShapeDtypeStruct((rows,heads*64),BF),jax.ShapeDtypeStruct((kp,heads*64),BF),jax.ShapeDtypeStruct((kp,heads*64),BF)],
        scratch_shapes=[pltpu.VMEM((2,rows,2*LANES),BF),pltpu.VMEM((2,rows,2*LANES),BF),pltpu.VMEM((kp,2*LANES),BF),
                        pltpu.VMEM((2,kp,LANES),BF),pltpu.VMEM((kp,2*LANES),BF),
                        pltpu.VMEM((kp,LANES),F32),pltpu.VMEM((kp,LANES),F32)],
        compiler_params=pltpu.CompilerParams(vmem_limit_bytes=60*2**20),
        cost_estimate=pair_cost(rows*kp*heads,5,12*rows*heads*64+8*kp*heads*64),
        name="cross_bwd",
    )(q,kv,kv,do,o,lse)


EPSILON = 1e-05
ROWS = 256
CHUNK = 768
BIG = 60 * 2**20


def whole(shape):
    return pl.BlockSpec(shape, lambda *_: (0,) * len(shape), pipeline_mode=pl.Buffered(1))


def by_rows(*lead_and_cols):
    *lead, cols = lead_and_cols
    return pl.BlockSpec((*lead, ROWS, cols), lambda i: (0,) * len(lead) + (i, 0))


def shaped(shape, dtype):
    return jax.ShapeDtypeStruct(shape, dtype)


def cost(flops, nbytes, trans=0):
    return pl.CostEstimate(flops=int(flops), bytes_accessed=int(nbytes), transcendentals=int(trans))


def normalize(values):
    centre = values - jnp.mean(values, -1, keepdims=True)
    scale = lax.rsqrt(jnp.mean(centre * centre, -1, keepdims=True) + EPSILON)
    return centre * scale, scale


def norm_grad(normed, scale, gain, grad):
    weighted = grad * gain
    return scale * (weighted - jnp.mean(weighted, -1, keepdims=True)
                    - normed * jnp.mean(weighted * normed, -1, keepdims=True))


def accumulate(ref, value):
    ref[...] = value + jnp.where(pl.program_id(0) == 0, jnp.zeros_like(value), ref[...])


def column_sum(values):
    return jnp.sum(values, 0, keepdims=True)


def qkv_heads(low, w_ref, bias_ref, at, out_ref):
    part = out_ref.shape[2]
    cols = nn(low, w_ref[at])
    out_ref[0] = ((cols[:, :part] + bias_ref[at, 0:1]) * (HEAD ** -0.5 * LOG2E)).astype(BF)
    out_ref[1] = cols[:, part:2 * part].astype(BF)
    out_ref[2] = (cols[:, 2 * part:] + bias_ref[at, 1:2]).astype(BF)


def qkv_sent_kernel(core_ref, x_ref, w_ref, gain_ref, shift_ref, bias_ref, norm_ref, sent_ref):
    normed, _ = normalize(x_ref[...].astype(F32))
    low = (normed * gain_ref[0:1] + shift_ref[0:1]).astype(BF)
    norm_ref[...] = low
    qkv_heads(low, w_ref, bias_ref, 1 - core_ref[0], sent_ref)


def qkv_kept_kernel(core_ref, norm_ref, w_ref, bias_ref, kept_ref):
    qkv_heads(norm_ref[...], w_ref, bias_ref, core_ref[0], kept_ref)


def qkv_sent(core, x, w, gain, shift, bias):
    rows, width = x.shape
    part = width // 2
    return pl.pallas_call(
        qkv_sent_kernel, grid=(rows // ROWS,),
        in_specs=[scalar(), by_rows(width), whole(w.shape), whole(gain.shape), whole(shift.shape), whole(bias.shape)],
        out_specs=[by_rows(width), by_rows(3, part)],
        out_shape=[shaped((rows, width), BF), shaped((3, rows, part), BF)],
        compiler_params=pltpu.CompilerParams(vmem_limit_bytes=BIG),
        cost_estimate=cost(3 * rows * width * width, 2 * (3 * width * width + 4 * rows * width)), name="qkv_sent",
    )(core, x, w, gain, shift, bias)


def qkv_kept(core, norm, w, bias):
    rows, width = norm.shape
    part = width // 2
    return pl.pallas_call(
        qkv_kept_kernel, grid=(rows // ROWS,),
        in_specs=[scalar(), by_rows(width), whole(w.shape), whole(bias.shape)],
        out_specs=by_rows(3, part), out_shape=shaped((3, rows, part), BF),
        compiler_params=pltpu.CompilerParams(vmem_limit_bytes=BIG),
        cost_estimate=cost(3 * rows * width * width, 2 * (3 * width * width + 3 * rows * width)), name="qkv_kept",
    )(core, norm, w, bias)


def memory_kernel(frames, mine_ref, own_ref, come_ref, w_ref, bias_ref, kv_ref, mem_ref):
    width = own_ref.shape[1]
    part = width // 2
    mem = jnp.where(mine_ref[0] == 1, own_ref[...], come_ref[...])
    row = lax.broadcasted_iota(jnp.int32, mem.shape, 0) + pl.program_id(0) * ROWS
    mem = jnp.where(row < frames, mem, jnp.zeros((), BF))
    mem_ref[...] = mem
    for t in range(2):
        cols = nn(mem, w_ref[t])
        kv_ref[:, t * part:(t + 1) * part] = cols[:, :part].astype(BF)
        kv_ref[:, width + t * part:width + (t + 1) * part] = (cols[:, part:] + bias_ref[4:5, t * part:(t + 1) * part]).astype(BF)


def memory_project(mine, own, come, w_mid, bias):
    frames, width = own.shape
    steps = pl.cdiv(frames, ROWS)
    return pl.pallas_call(
        functools.partial(memory_kernel, frames), grid=(steps,),
        in_specs=[scalar(), by_rows(width), by_rows(width),
                  pl.BlockSpec((2, width, width), lambda i: (0, 0, 1), pipeline_mode=pl.Buffered(1)), whole(bias.shape)],
        out_specs=[by_rows(2 * width), by_rows(width)],
        out_shape=[shaped((steps * ROWS, 2 * width), BF), shaped((steps * ROWS, width), BF)],
        compiler_params=pltpu.CompilerParams(vmem_limit_bytes=BIG),
        cost_estimate=cost(4 * frames * width * width, 2 * (2 * width * width + 5 * frames * width)), name="memory_project",
    )(mine, own, come, w_mid, bias)


def middle_kernel(core_ref, x_ref, own_ref, come_ref, wo_ref, wq_ref, gain_ref, shift_ref, bias_ref,
                  resid_ref, norm_ref, q_ref):
    part = own_ref.shape[1]
    core = core_ref[0]
    resid = x_ref[...].astype(F32) + nt(own_ref[...], wo_ref[core]) + nt(come_ref[...], wo_ref[1 - core]) + bias_ref[2:3]
    resid_ref[...] = resid
    normed, _ = normalize(resid)
    low = (normed * gain_ref[1:2] + shift_ref[1:2]).astype(BF)
    norm_ref[...] = low
    for t in range(2):
        at = slice(t * part, (t + 1) * part)
        q_ref[:, at] = ((nn(low, wq_ref[t]) + bias_ref[3:4, at]) * (HEAD ** -0.5 * LOG2E)).astype(BF)


def middle(core, x, own, come, w_mid, gain, shift, bias):
    rows, width = x.shape
    part = width // 2
    w_at = lambda c: pl.BlockSpec((2, width, part), lambda i: (0, 0, c), pipeline_mode=pl.Buffered(1))
    return pl.pallas_call(
        middle_kernel, grid=(rows // ROWS,),
        in_specs=[scalar(), by_rows(width), by_rows(part), by_rows(part), w_at(0), w_at(1),
                  whole(gain.shape), whole(shift.shape), whole(bias.shape)],
        out_specs=[by_rows(width)] * 3,
        out_shape=[shaped((rows, width), F32), shaped((rows, width), BF), shaped((rows, width), BF)],
        compiler_params=pltpu.CompilerParams(vmem_limit_bytes=BIG),
        cost_estimate=cost(4 * rows * width * width, 4 * width * width + 12 * rows * width), name="middle",
    )(core, x, own, come, w_mid, w_mid, gain, shift, bias)


def gelu_parts(v):
    z = jnp.abs(v) * (0.5 ** 0.5)
    t = 1.0 / (1.0 + 0.3275911 * z)
    bell = jnp.exp2(v * v * (-0.5 * LOG2E))
    poly = ((((1.061405429 * t - 1.453152027) * t + 1.421413741) * t - 0.284496736) * t + 0.254829592) * t
    tail = (0.5 * poly) * bell
    phi = jnp.where(v >= 0, 1.0 - tail, tail)
    return phi, phi + v * bell * 0.3989422804014327


def feed_kernel(mine_ref, attn_ref, resid_ref, g_own_ref, g_come_ref, wo_ref, wi_ref, wm_ref, gain_ref, shift_ref, bias_ref, unit_bias_ref, out_bias_ref,
                out_ref, norm_ref, hidden_ref, dpre_ref, g2_ref, dattn_ref, g_ref,
                sum_g_ref, sum_dpre_ref, sum_g2_ref, sum_gain_ref, sum_shift_ref):
    part = wo_ref.shape[2]
    units = wi_ref.shape[2]
    resid = resid_ref[...] + bias_ref[5:6]
    for t in range(2):
        resid = resid + nt(attn_ref[:, t * part:(t + 1) * part], wo_ref[t])
    normed, scale = normalize(resid)
    low = (normed * gain_ref[2:3] + shift_ref[2:3]).astype(BF)
    norm_ref[...] = low
    g_low = jnp.where(mine_ref[0] == 1, g_own_ref[...], g_come_ref[...])
    g_ref[...] = g_low
    out = resid + out_bias_ref[...]
    back = jnp.zeros_like(resid)
    sums = []
    spots = [(t, c) for t in range(2) for c in range(0, units, CHUNK)]

    def first(spot):
        t, c = spot
        at = slice(t * units + c, t * units + c + CHUNK)
        return nn(low, wi_ref[t, :, c:c + CHUNK]) + unit_bias_ref[:, at], nn(g_low, wm_ref[t, :, c:c + CHUNK])

    ahead = first(spots[0])
    for k, (t, c) in enumerate(spots):
        at = slice(t * units + c, t * units + c + CHUNK)
        pre, back_hidden = ahead
        if k + 1 < len(spots):
            ahead = first(spots[k + 1])
        phi, slope = gelu_parts(pre)
        hidden = (pre * phi).astype(BF)
        hidden_ref[:, at] = hidden
        out = out + nt(hidden, wm_ref[t, :, c:c + CHUNK])
        dpre = back_hidden * slope
        sums.append(column_sum(dpre))
        dpre = dpre.astype(BF)
        dpre_ref[:, at] = dpre
        back = back + nt(dpre, wi_ref[t, :, c:c + CHUNK])
    out_ref[...] = out.astype(BF)
    sums = jnp.concatenate(sums, 1)
    wide = sum_dpre_ref.shape[1]
    accumulate(sum_dpre_ref, jnp.concatenate([sums[:, i * wide:(i + 1) * wide] for i in range(sum_dpre_ref.shape[0])], 0))
    g = g_low.astype(F32)
    accumulate(sum_g_ref, column_sum(g))
    accumulate(sum_gain_ref, column_sum(back * normed))
    accumulate(sum_shift_ref, column_sum(back))
    g2 = g + norm_grad(normed, scale, gain_ref[2:3], back)
    accumulate(sum_g2_ref, column_sum(g2))
    g2_ref[...] = g2
    g2_low = g2.astype(BF)
    for t in range(2):
        dattn_ref[:, t * part:(t + 1) * part] = nn(g2_low, wo_ref[t]).astype(BF)


def feed(mine, attn, resid, g_own, g_come, w_mid, w_ff, gain, shift, bias, unit_bias, out_bias):
    rows, width = resid.shape
    part = width // 2
    units = w_ff.shape[2] // 2
    w_at = lambda cols, c: pl.BlockSpec((2, width, cols), lambda i: (0, 0, c), pipeline_mode=pl.Buffered(1))
    line = lambda count: (pl.BlockSpec((count, width), lambda i: (0, 0)), shaped((count, width), F32))
    lines = [line(1), line(2 * units // width), line(1), line(1), line(1)]
    return pl.pallas_call(
        feed_kernel, grid=(rows // ROWS,),
        in_specs=[scalar(), by_rows(width), by_rows(width), by_rows(width), by_rows(width), w_at(part, 4), w_at(units, 0), w_at(units, 1),
                  whole(gain.shape), whole(shift.shape), whole(bias.shape), whole(unit_bias.shape), whole(out_bias.shape)],
        out_specs=[by_rows(width), by_rows(width), by_rows(2 * units), by_rows(2 * units), by_rows(width), by_rows(width), by_rows(width)] + [a for a, _ in lines],
        out_shape=[shaped((rows, width), BF), shaped((rows, width), BF), shaped((rows, 2 * units), BF), shaped((rows, 2 * units), BF),
                   shaped((rows, width), F32), shaped((rows, width), BF), shaped((rows, width), BF)] + [b for _, b in lines],
        compiler_params=pltpu.CompilerParams(vmem_limit_bytes=BIG),
        cost_estimate=cost(2 * rows * width * (2 * width + 8 * units), 2 * width * (width + 4 * units) + 2 * rows * (8 * width + 4 * units), 4 * rows * units),
        name="feed",
    )(mine, attn, resid, g_own, g_come, w_mid, w_ff, w_ff, gain, shift, bias, unit_bias, out_bias)


def feed_weights_kernel(norm_ref, g_ref, dpre_ref, hidden_ref, out_ref):
    cols = dpre_ref.shape[1]
    out_ref[0, :, :cols] = tn(norm_ref[...], dpre_ref[...]).astype(BF)
    out_ref[0, :, cols:] = tn(g_ref[...], hidden_ref[...]).astype(BF)


def feed_weights(norm, g, dpre, hidden):
    rows, width = norm.shape
    units = dpre.shape[1] // 2
    cols = units // 2
    return pl.pallas_call(
        feed_weights_kernel, grid=(2, 2),
        in_specs=[whole(norm.shape), whole(g.shape), pl.BlockSpec((rows, cols), lambda t, c: (0, 2 * t + c)),
                  pl.BlockSpec((rows, cols), lambda t, c: (0, 2 * t + c))],
        out_specs=pl.BlockSpec((1, width, 2 * cols), lambda t, c: (t, 0, c)),
        out_shape=shaped((2, width, 2 * units), BF),
        compiler_params=pltpu.CompilerParams(vmem_limit_bytes=BIG),
        cost_estimate=cost(8 * rows * width * units, 2 * (4 * width * units + 4 * rows * units)), name="feed_weights",
    )(norm, g, dpre, hidden)


def middle_back_kernel(core_ref, dq_ref, resid_ref, g2_ref, wq_ref, wo_ref, gain_ref,
                       g1_ref, kept_ref, sent_ref, sum_dq_ref, sum_g1_ref, sum_gain_ref, sum_shift_ref):
    part = kept_ref.shape[1]
    core = core_ref[0]
    dq = dq_ref[...]
    back = nt(dq[:, :part], wq_ref[0]) + nt(dq[:, part:], wq_ref[1])
    accumulate(sum_dq_ref, column_sum(dq.astype(F32)))
    normed, scale = normalize(resid_ref[...])
    accumulate(sum_gain_ref, column_sum(back * normed))
    accumulate(sum_shift_ref, column_sum(back))
    g1 = g2_ref[...] + norm_grad(normed, scale, gain_ref[1:2], back)
    g1_ref[...] = g1
    accumulate(sum_g1_ref, column_sum(g1))
    low = g1.astype(BF)
    kept_ref[...] = nn(low, wo_ref[core]).astype(BF)
    sent_ref[...] = nn(low, wo_ref[1 - core]).astype(BF)


def middle_back(core, dq, resid, g2, w_mid, gain):
    rows, width = resid.shape
    part = width // 2
    w_at = lambda c: pl.BlockSpec((2, width, part), lambda i: (0, 0, c), pipeline_mode=pl.Buffered(1))
    line = pl.BlockSpec((1, width), lambda i: (0, 0))
    return pl.pallas_call(
        middle_back_kernel, grid=(rows // ROWS,),
        in_specs=[scalar(), by_rows(width), by_rows(width), by_rows(width), w_at(1), w_at(0), whole(gain.shape)],
        out_specs=[by_rows(width), by_rows(part), by_rows(part)] + [line] * 4,
        out_shape=[shaped((rows, width), F32), shaped((rows, part), BF), shaped((rows, part), BF)] + [shaped((1, width), F32)] * 4,
        compiler_params=pltpu.CompilerParams(vmem_limit_bytes=BIG),
        cost_estimate=cost(4 * rows * width * width, 4 * width * width + 18 * rows * width), name="middle_back",
    )(core, dq, resid, g2, w_mid, w_mid, gain)


def middle_weights_kernel(core_ref, g1_ref, own_ref, come_ref, norm_ref, dq_ref, mem_ref, dk_ref, dv_ref, g2_ref, attn_ref,
                          out_ref, sum_dv_ref):
    part = own_ref.shape[1]
    attn_self = jnp.where(pl.program_id(0) == core_ref[0], own_ref[...], come_ref[...])
    out_ref[0, :, :part] = tn(g1_ref[...].astype(BF), attn_self).astype(BF)
    out_ref[0, :, part:2 * part] = tn(norm_ref[...], dq_ref[...]).astype(BF)
    mem = mem_ref[...]
    out_ref[0, :, 2 * part:3 * part] = tn(mem, dk_ref[...]).astype(BF)
    out_ref[0, :, 3 * part:4 * part] = tn(mem, dv_ref[...]).astype(BF)
    out_ref[0, :, 4 * part:] = tn(g2_ref[...].astype(BF), attn_ref[...]).astype(BF)
    sum_dv_ref[...] = column_sum(dv_ref[...].astype(F32))


def middle_weights(core, g1, own, come, norm, dq, mem, dk, dv, g2, attn):
    rows, width = norm.shape
    frames = mem.shape[0]
    part = width // 2
    half = lambda n: pl.BlockSpec((n, part), lambda t: (0, t))
    return pl.pallas_call(
        middle_weights_kernel, grid=(2,),
        in_specs=[scalar(), whole(g1.shape), whole(own.shape), whole(come.shape), whole(norm.shape), half(rows), whole(mem.shape),
                  half(frames), half(frames), whole(g2.shape), half(rows)],
        out_specs=[pl.BlockSpec((1, width, 5 * part), lambda t: (t, 0, 0)), pl.BlockSpec((1, part), lambda t: (0, t))],
        out_shape=[shaped((2, width, 5 * part), BF), shaped((1, width), F32)],
        compiler_params=pltpu.CompilerParams(vmem_limit_bytes=BIG),
        cost_estimate=cost(2 * width * width * (3 * rows + 2 * frames), 10 * width * width + 2 * width * (10 * rows + 3 * frames)),
        name="middle_weights",
    )(core, g1, own, come, norm, dq, mem, dk, dv, g2, attn)


def qkv_back_kernel(core_ref, own_ref, come_ref, x_ref, g1_ref, w_ref, gain_ref, grad_ref, sum_gain_ref, sum_shift_ref):
    part = own_ref.shape[2]
    core = core_ref[0]
    back = jnp.zeros(x_ref.shape, F32)
    for ref, at in ((own_ref, core), (come_ref, 1 - core)):
        for j in range(3):
            back = back + nt(ref[j], w_ref[at, :, j * part:(j + 1) * part])
    normed, scale = normalize(x_ref[...].astype(F32))
    accumulate(sum_gain_ref, column_sum(back * normed))
    accumulate(sum_shift_ref, column_sum(back))
    grad_ref[...] = (g1_ref[...] + norm_grad(normed, scale, gain_ref[0:1], back)).astype(BF)


def qkv_back(core, own, come, x, g1, w, gain):
    rows, width = x.shape
    part = width // 2
    line = pl.BlockSpec((1, width), lambda i: (0, 0))
    return pl.pallas_call(
        qkv_back_kernel, grid=(rows // ROWS,),
        in_specs=[scalar(), by_rows(3, part), by_rows(3, part), by_rows(width), by_rows(width), whole(w.shape), whole(gain.shape)],
        out_specs=[by_rows(width), line, line],
        out_shape=[shaped((rows, width), BF), shaped((1, width), F32), shaped((1, width), F32)],
        compiler_params=pltpu.CompilerParams(vmem_limit_bytes=BIG),
        cost_estimate=cost(6 * rows * width * width, 2 * (3 * width * width + 7 * rows * width)), name="qkv_back",
    )(core, own, come, x, g1, w, gain)


def qkv_weights_kernel(core_ref, norm_ref, own_ref, come_ref, out_ref, sum_q_ref, sum_v_ref):
    part = own_ref.shape[2]
    mine = pl.program_id(0) == core_ref[0]
    norm = norm_ref[...]
    for j in range(3):
        grad = jnp.where(mine, own_ref[j], come_ref[j])
        out_ref[0, :, j * part:(j + 1) * part] = tn(norm, grad).astype(BF)
        if j != 1:
            (sum_q_ref if j == 0 else sum_v_ref)[...] = column_sum(grad.astype(F32))


def qkv_weights(core, norm, own, come):
    rows, width = norm.shape
    part = width // 2
    return pl.pallas_call(
        qkv_weights_kernel, grid=(2,),
        in_specs=[scalar(), whole(norm.shape), whole(own.shape), whole(come.shape)],
        out_specs=[pl.BlockSpec((1, width, 3 * part), lambda t: (t, 0, 0)), pl.BlockSpec((1, part), lambda t: (0, t)), pl.BlockSpec((1, part), lambda t: (0, t))],
        out_shape=[shaped((2, width, 3 * part), BF), shaped((1, width), F32), shaped((1, width), F32)],
        compiler_params=pltpu.CompilerParams(vmem_limit_bytes=BIG),
        cost_estimate=cost(6 * rows * width * width, 2 * (3 * width * width + 4 * rows * width)), name="qkv_weights",
    )(core, norm, own, come)


def bit_names(chips):
    return ["t"] + ["k%d" % b for b in reversed(range((chips - 1).bit_length()))] + ["core"]


def my_bit(name):
    if name == "t":
        return lax.axis_index("tensor")
    if name == "core":
        return lax.axis_index("core")
    return lax.axis_index("chip") // 2 ** int(name[1:]) % 2


def partner(name):
    bit = my_bit(name)
    if name == "t":
        return {"tensor": 1 - bit}
    if name == "core":
        return {"core": 1 - bit}
    return {"chip": lax.axis_index("chip") + 2 ** int(name[1:]) * (1 - 2 * bit)}


def greet(names, *others):
    barrier = pltpu.get_barrier_semaphore()
    for device in [partner(name) for name in names] + list(others):
        pl.semaphore_signal(barrier, inc=1, device_id=device, device_id_type=pl.DeviceIdType.MESH)
    pl.semaphore_wait(barrier, len(names) + len(others))


def exchange_orders(names):
    low = [n for n in reversed(names) if n[0] == "k"]
    return [["core", "t"] + low, ["core"] + low + ["t"], ["core"] + low[1:] + ["t"] + low[:1]]


def stream_cols(cols, count):
    tiles = cols // LANES
    cuts = [tiles * i // count * LANES for i in range(count + 1)]
    return [slice(a, b) for a, b in zip(cuts, cuts[1:])]


def gather_kernel(names, orders, own_ref, seg_ref, x_ref, out_ref, seg_out_ref, moved_ref, block, segs, local_sem, send_sem, recv_sem):
    core, tensor = lax.axis_index("core"), lax.axis_index("tensor")
    greet(names, {"core": 1 - core, "tensor": 1 - tensor})
    spare = len(orders)
    swap = pltpu.make_async_remote_copy(x_ref, moved_ref, send_sem.at[spare, 2], recv_sem.at[spare, 2],
                                        device_id={"core": tensor, "tensor": core}, device_id_type=pl.DeviceIdType.MESH)
    stay = pltpu.make_async_copy(x_ref, moved_ref, local_sem.at[1])

    @pl.when(core != tensor)
    def _():
        swap.start()

    @pl.when(core == tensor)
    def _():
        stay.start()

    pieces, _, part = own_ref.shape
    for i in range(pieces):
        block[:, i * part:(i + 1) * part] = own_ref[i]
    lanes = stream_cols(block.shape[1], len(orders))
    place = tuple(my_bit(n) for n in names)
    known = [[] for _ in orders]
    sent = []
    flying = [None] * len(orders)

    def send(src, dst, st, step, name):
        copy = pltpu.make_async_remote_copy(src, dst, send_sem.at[st, step], recv_sem.at[st, step],
                                            device_id=partner(name), device_id_type=pl.DeviceIdType.MESH)
        copy.start()
        sent.append(copy)
        return copy

    def start(st, step):
        name = orders[st][step]
        at = tuple(slice(None) if n in known[st] else my_bit(n) for n in names)
        dst = out_ref.at[at + (slice(None), lanes[st])]
        flying[st] = send(dst if step else block.at[:, lanes[st]], dst, st, step, name)
        known[st].append(name)

    for st in range(len(orders)):
        start(st, 0)
    local = pltpu.make_async_copy(block, out_ref.at[place], local_sem.at[0])
    local.start()
    segs[core, tensor] = seg_ref[...]
    along = send(segs.at[core, tensor], segs.at[core, tensor], spare, 0, "t")
    local.wait()
    for step in range(len(names)):
        for st in range(len(orders)):
            flying[st].wait_recv()
            if step + 1 < len(names):
                start(st, step + 1)
        if step == 0:
            along.wait_recv()
            along = send(segs.at[core], segs.at[core], spare, 1, "core")
    along.wait_recv()
    seg_out_ref[...] = segs[tensor, 1]
    for copy in sent:
        copy.wait_send()

    @pl.when(core != tensor)
    def _():
        swap.wait()

    @pl.when(core == tensor)
    def _():
        stay.wait()


def gather_all(shard, seg, x, chips):
    names = bit_names(chips)
    orders = [list(reversed(o)) for o in exchange_orders(names)]
    pieces, rows, part = shard.shape
    cols = pieces * part
    dma = pltpu.SemaphoreType.DMA
    vmem = pl.BlockSpec(memory_space=pltpu.VMEM)
    seg = seg.reshape(-1, LANES)
    hbm = pl.BlockSpec(memory_space=pl.ANY)
    full, seg, moved = pl.pallas_call(
        functools.partial(gather_kernel, names, orders),
        in_specs=[vmem, vmem, hbm], out_specs=[hbm, vmem, hbm],
        out_shape=[shaped((2,) * len(names) + (rows, cols), shard.dtype), shaped(seg.shape, seg.dtype), shaped(x.shape, x.dtype)],
        scratch_shapes=[pltpu.VMEM((rows, cols), shard.dtype), pltpu.VMEM((2, 2) + seg.shape, seg.dtype),
                        dma((2,)), dma((len(orders) + 1, len(names))), dma((len(orders) + 1, len(names)))],
        compiler_params=pltpu.CompilerParams(collective_id=0, has_side_effects=True, vmem_limit_bytes=BIG),
        cost_estimate=cost(0, 1e6), name="gather_all",
    )(shard, seg, x)
    return full.reshape(2, -1, cols), seg.reshape(-1), moved


class Sums:
    def __init__(self, names, send_sem, recv_sem):
        self.names, self.sems, self.streams = names, (send_sem, recv_sem), []

    def add(self, sent_ref, kept_ref, order, recv, held, out):
        self.streams.append(dict(sent=sent_ref, kept=kept_ref, order=order, recv=recv, held=held, out=out, left=list(self.names),
                                 step=0, copies=[]))
        return len(self.streams) - 1

    def start(self, k):
        s = self.streams[k]
        name = s["order"][s["step"]]
        src = s["sent"] if s["kept"] is None else s["sent"].at[tuple(1 - my_bit(n) if n == name else slice(None) for n in s["left"])]
        copy = pltpu.make_async_remote_copy(src, s["recv"][s["step"]], self.sems[0].at[k, s["step"]], self.sems[1].at[k, s["step"]],
                                            device_id=partner(name), device_id_type=pl.DeviceIdType.MESH)
        copy.start()
        s["copies"].append(copy)

    def advance(self, k):
        s = self.streams[k]
        step = s["step"]
        if step == len(self.names):
            return
        s["copies"][-1].wait_recv()
        name = s["order"][step]
        if s["kept"] is None:
            total = s["sent"][...] + s["recv"][step][...]
        else:
            kept = s["kept"].at[tuple(my_bit(n) if n == name else slice(None) for n in s["left"])]
            total = kept[...].astype(F32) + s["recv"][step][...].astype(F32)
            s["left"].remove(name)
        s["step"] += 1
        if s["step"] == len(self.names):
            s["out"](total)
            return
        held = s["held"][step]
        held[...] = total.astype(held.dtype)
        if s["kept"] is not None:
            s["kept"] = held
        s["sent"] = held
        self.start(k)

    def finish(self):
        for _ in self.names:
            for k in range(len(self.streams)):
                self.advance(k)
        for s in self.streams:
            for copy in s["copies"]:
                copy.wait_send()


def part_streams(cols, part, count):
    return [slice(a.start * part, a.stop * part) for a in stream_parts(cols // part, count)]


def stream_parts(parts, count):
    cuts = [parts * i // count for i in range(count + 1)]
    return [slice(a, b) for a, b in zip(cuts, cuts[1:])]


def sum_bufs(steps, rows, lanes):
    recv = [pltpu.VMEM((2,) * (steps - 1 - i) + (rows, lane.stop - lane.start), BF) for lane in lanes for i in range(steps)]
    held = [pltpu.VMEM((2,) * (steps - 1 - i) + (rows, lane.stop - lane.start), BF) for lane in lanes for i in range(steps - 1)]
    return recv + held


def split_bufs(bufs, steps, count):
    recv, held = bufs[:count * steps], bufs[count * steps:]
    return [(recv[st * steps:(st + 1) * steps], held[st * (steps - 1):(st + 1) * (steps - 1)]) for st in range(count)]


def put_pieces(lane, part, place):
    def out(total):
        for at in range(lane.start, lane.stop, part):
            place(at // part, total[:, at - lane.start:at - lane.start + part])
    return out


def unpack_ff(ff_ref, ff_in_ref, ff_out_ref):
    quarter = ff_ref.shape[1] // 4
    for i in range(4):
        ref, at = (ff_out_ref if i % 2 else ff_in_ref), i // 2 * quarter
        ref[:, at:at + quarter] = ff_ref[:, i * quarter:(i + 1) * quarter].astype(F32)


def fill_rows(ref, values):
    row = 0
    for value in values:
        ref[row:row + value.shape[0]] = value
        row += value.shape[0]
    if row < ref.shape[0]:
        ref[row:] = jnp.zeros((ref.shape[0] - row, ref.shape[1]), F32)


def sum_kernel(names, orders, lanes, smalls, pieces, grad_ref, ff_ref, *refs):
    small_refs, refs = refs[:smalls], refs[smalls:]
    qkv_ref, *out_refs = refs[:pieces + 1]
    small_out_ref, ff_in_ref, ff_out_ref, small_first, small_recv, small_held, send_sem, recv_sem, *bufs = refs[pieces + 1:]
    greet(names)
    steps = len(names)

    def place(i, value):
        if i < 3:
            qkv_ref[i] = value
        else:
            out_refs[i - 3][...] = value

    def small_out(total):
        small_out_ref[...] = total

    sums = Sums(names, send_sem, recv_sem)
    part = qkv_ref.shape[2]
    for lane, order, (recv, held) in zip(lanes, orders, split_bufs(bufs, steps, len(lanes))):
        ref = grad_ref.at[(slice(None),) * (steps + 1) + (lane,)]
        sums.start(sums.add(ref, ref, order, recv, held, put_pieces(lane, part, place)))
    fill_rows(small_first, [ref[...] for ref in small_refs])
    sums.start(sums.add(small_first, None, orders[0], [small_recv.at[i] for i in range(steps)],
                        [small_held.at[i] for i in range(steps - 1)], small_out))
    unpack_ff(ff_ref, ff_in_ref, ff_out_ref)
    sums.finish()


def small_bufs(steps, small):
    shape = ((sum(s.shape[0] for s in small) + 7) // 8 * 8, small[-1].shape[1])
    return shape, [pltpu.VMEM(shape, F32), pltpu.VMEM((steps,) + shape, F32), pltpu.VMEM((steps,) + shape, F32)]


def sum_all(grad, ff, small, chips):
    names = bit_names(chips)
    orders = exchange_orders(names)
    cols = grad.shape[2]
    rows = grad.shape[1] // (2 * chips)
    steps = len(names)
    part = small[0].shape[1] // 2
    pieces = cols // part - 3
    lanes = part_streams(cols, part, len(orders))
    shape, extra = small_bufs(steps, small)
    dma = pltpu.SemaphoreType.DMA
    vmem = pl.BlockSpec(memory_space=pltpu.VMEM)
    return pl.pallas_call(
        functools.partial(sum_kernel, names, orders, lanes, len(small), pieces),
        in_specs=[vmem] * (2 + len(small)), out_specs=[vmem] * (pieces + 4),
        out_shape=[shaped((3, rows, part), F32)] + [shaped((rows, part), F32)] * pieces
        + [shaped(shape, F32)] + [shaped((rows, ff.shape[1] // 2), F32)] * 2,
        scratch_shapes=extra + [dma((len(orders) + 1, steps)), dma((len(orders) + 1, steps))] + sum_bufs(steps, rows, lanes),
        compiler_params=pltpu.CompilerParams(collective_id=1, has_side_effects=True, vmem_limit_bytes=BIG),
        cost_estimate=cost(0, 1e6), name="sum_all",
    )(grad.reshape((2,) * steps + (rows, cols)), ff, *small)


def end_kernel(names, orders, mid_lanes, qkv_lanes, smalls, mid_hbm, kept_hbm, come_hbm, x_hbm, norm_hbm, g1_hbm, w_hbm,
               gain_ref, ff_ref, *refs):
    small_refs, refs = refs[:smalls], refs[smalls:]
    qkv_ref, refs = refs[0], refs[1:]
    pieces = len(mid_lanes)
    parts = mid_hbm.shape[-1] // qkv_ref.shape[2]
    mid_refs, refs = refs[:parts], refs[parts:]
    (small_out_ref, ff_in_ref, ff_out_ref, moved_ref, mid, kept, come, x, norm, g1, w, grad_qkv, grad_low, small_first, small_recv,
     small_held, load_sem, send_sem, recv_sem, *bufs) = refs
    core, tensor = lax.axis_index("core"), lax.axis_index("tensor")
    steps = len(names)
    part = qkv_ref.shape[2]
    loads = [pltpu.make_async_copy(src, dst, load_sem.at[i]) for i, (src, dst) in enumerate(
        ((mid_hbm, mid), (w_hbm, w), (kept_hbm, kept), (come_hbm, come), (x_hbm, x), (g1_hbm, g1), (norm_hbm, norm)))]
    for load in loads[1:] + loads[:1]:
        load.start()
    greet(names, {"core": 1 - core, "tensor": 1 - tensor})
    sums = Sums(names, send_sem, recv_sem)
    split = len(mid_lanes) * (2 * steps - 1)
    everything = (slice(None),) * (steps + 1)

    def mid_place(i, value):
        mid_refs[i][...] = value

    def qkv_place(i, value):
        qkv_ref[i] = value

    def small_out(total):
        small_out_ref[...] = total

    for lane, order, (recv, held) in zip(mid_lanes, orders, split_bufs(bufs[:split], steps, len(mid_lanes))):
        at = everything + (lane,)
        sums.start(sums.add(mid_hbm.at[at], mid.at[at], order, recv, held, put_pieces(lane, part, mid_place)))

    def step_mid():
        for k in range(pieces):
            sums.advance(k)

    for load in loads[1:6]:
        load.wait()
    rows, width = x.shape
    gains, shifts = 0.0, 0.0
    for b in range(rows // ROWS):
        at = slice(b * ROWS, (b + 1) * ROWS)
        back = jnp.zeros((ROWS, width), F32)
        for ref, t in ((kept, core), (come, 1 - core)):
            for j in range(3):
                back = back + nt(ref[j, at, :], w[t, :, j * part:(j + 1) * part])
        normed, scale = normalize(x[at, :].astype(F32))
        gains = gains + column_sum(back * normed)
        shifts = shifts + column_sum(back)
        grad_low[at, :] = (g1[at, :] + norm_grad(normed, scale, gain_ref[0:1], back)).astype(BF)
        if b == 1:
            loads[0].wait()
            step_mid()
    spare = len(sums.streams) + len(qkv_lanes) + 1
    swap = pltpu.make_async_remote_copy(grad_low, moved_ref, send_sem.at[spare, 0], recv_sem.at[spare, 0],
                                        device_id={"core": tensor, "tensor": core}, device_id_type=pl.DeviceIdType.MESH)
    stay = pltpu.make_async_copy(grad_low, moved_ref, load_sem.at[7])

    @pl.when(core != tensor)
    def _():
        swap.start()

    @pl.when(core == tensor)
    def _():
        stay.start()

    step_mid()
    loads[6].wait()
    bias = []
    for ref, t in ((kept, core), (come, 1 - core)):
        for j in range(3):
            grad = tn(norm[...], ref[j]).astype(BF)
            grad_qkv[(t,) + everything[1:] + (slice(j * part, (j + 1) * part),)] = grad.reshape(grad_qkv.shape[1:-1] + (part,))
            bias.append(column_sum(ref[j].astype(F32)))
        step_mid()
    for lane, order, (recv, held) in zip(qkv_lanes, orders, split_bufs(bufs[split:], steps, len(qkv_lanes))):
        ref = grad_qkv.at[everything + (lane,)]
        sums.start(sums.add(ref, ref, order, recv, held, put_pieces(lane, part, qkv_place)))

    def line(j):
        return jnp.concatenate([jnp.where(core == 0, bias[j], bias[3 + j]), jnp.where(core == 0, bias[3 + j], bias[j])], 1)

    small = [ref[...] for ref in small_refs]
    fill_rows(small_first, [gains, *small[:2], shifts, *small[2:4], line(0), line(2), *small[4:]])
    sums.start(sums.add(small_first, None, orders[0], [small_recv.at[i] for i in range(steps)],
                        [small_held.at[i] for i in range(steps - 1)], small_out))
    unpack_ff(ff_ref, ff_in_ref, ff_out_ref)
    sums.finish()

    @pl.when(core != tensor)
    def _():
        swap.wait()

    @pl.when(core == tensor)
    def _():
        stay.wait()


def end_all(mid, kept, come, x, norm, g1, w, gain, ff, small, chips):
    names = bit_names(chips)
    orders = exchange_orders(names)
    steps = len(names)
    rows, width = x.shape
    part = width // 2
    here = width // (2 * chips)
    mid_cols = mid.shape[2]
    mid_lanes = part_streams(mid_cols, part, len(orders))
    qkv_lanes = part_streams(3 * part, part, len(orders))
    pieces = mid_cols // part
    shape, extra = small_bufs(steps, small + [jnp.zeros((4, width), F32)])
    dma = pltpu.SemaphoreType.DMA
    vmem, hbm = pl.BlockSpec(memory_space=pltpu.VMEM), pl.BlockSpec(memory_space=pl.ANY)
    lead = (2,) * steps
    mid = mid.reshape(lead + (here, mid_cols))
    count = len(orders) * 2 + 2
    return pl.pallas_call(
        functools.partial(end_kernel, names, orders, mid_lanes, qkv_lanes, len(small)),
        in_specs=[hbm] * 7 + [vmem] * (2 + len(small)), out_specs=[vmem] * (pieces + 4) + [hbm],
        out_shape=[shaped((3, here, part), F32)] + [shaped((here, part), F32)] * pieces
        + [shaped(shape, F32)] + [shaped((here, ff.shape[1] // 2), F32)] * 2 + [shaped((rows, width), BF)],
        scratch_shapes=[pltpu.VMEM(v.shape, v.dtype) for v in (mid, kept, come, x, norm, g1, w)]
        + [pltpu.VMEM(lead + (here, 3 * part), BF), pltpu.VMEM((rows, width), BF)] + extra
        + [dma((8,)), dma((count, steps)), dma((count, steps))]
        + sum_bufs(steps, here, mid_lanes) + sum_bufs(steps, here, qkv_lanes),
        compiler_params=pltpu.CompilerParams(collective_id=1, has_side_effects=True, vmem_limit_bytes=BIG),
        cost_estimate=cost(0, 1e6), name="end_all",
    )(mid, kept, come, x, norm, g1, w, gain, ff, *small)


ALL = ("tensor", "chip", "core")


def fetch(shard):
    full = lax.all_gather(shard, ALL, axis=0, tiled=True)
    return full.reshape(2, -1, shard.shape[1])


def spread_sum(grad):
    return lax.psum_scatter(grad.reshape(-1, grad.shape[2]), ALL, scatter_dimension=0, tiled=True)


def on_device(tokens, memory, seg_ids, positions, grad_output, attn_in, attn_out, cross_q, cross_kv,
              cross_out, mlp_in, mlp_out, norm_gain, norm_bias, proj_bias, mlp_bias, out_bias):
    width = tokens.shape[1]
    rows_here, _, part = attn_in.shape
    units = mlp_in.shape[1]
    heads = width // HEAD
    frames = memory.shape[1]
    core = lax.axis_index("core")
    tensor = lax.axis_index("tensor")
    core_at = core.astype(jnp.int32).reshape(1)
    swap = [(0, 0), (1, 2), (2, 1), (3, 3)]
    mine = (core == tensor).astype(jnp.int32).reshape(1)
    fix = lambda x: lax.ppermute(x, ("core", "tensor"), swap)
    other = lambda x: lax.ppermute(x, "core", [(0, 1), (1, 0)])

    chips = lax.axis_size("chip")
    mid = jnp.concatenate([attn_out.T, cross_q, cross_kv.reshape(rows_here, 2 * part), cross_out.T], 1)
    first, mid = lax.optimization_barrier((attn_in.transpose(1, 0, 2), mid))
    w_mid = fetch(mid)
    w_qkv, seg_cont, moved = gather_all(first, seg_ids, tokens, chips)
    late_in, late_out, w_qkv = lax.optimization_barrier((mlp_in, mlp_out, w_qkv))
    w_ff = fetch(jnp.concatenate([late_in, late_out.T], 1))
    bias_halves = proj_bias[:2].reshape(2, 2, part).transpose(1, 0, 2)

    norm_one, sent = qkv_sent(core_at, moved, w_qkv, norm_gain, norm_bias, bias_halves)
    come = other(sent)
    kept = qkv_kept(core_at, norm_one, w_qkv, bias_halves)
    grad_come = lax.ppermute(grad_output, ("core", "tensor"), [(1, 2), (2, 1)])
    mem_come = other(memory[0])
    o_kept, o_sent, lse_self = self_fwd(core_at, kept, come, seg_cont[:, None], seg_cont[None, :])
    o_come = other(o_sent)
    kv, mem = memory_project(mine, memory[0], mem_come, w_mid, proj_bias)
    kv, o_come = lax.optimization_barrier((kv, o_come))
    resid_one, norm_two, q_cross = middle(core_at, moved, o_kept, o_come, w_mid, norm_gain, norm_bias, proj_bias)
    attn_cross, lse_cross = cross_fwd(q_cross, kv, frames, heads)
    (out, norm_three, hidden, dpre, g_two, dattn, grad_in, sum_g, sum_dpre, sum_g_two, gain_three, shift_three) = feed(
        mine, attn_cross, resid_one, grad_output, grad_come, w_mid, w_ff, norm_gain, norm_bias, proj_bias, mlp_bias[None], out_bias[None])
    output = fix(out)
    gw_ff = feed_weights(norm_three, grad_in, dpre, hidden)
    dattn, gw_ff = lax.optimization_barrier((dattn, gw_ff))
    g_ff = spread_sum(gw_ff)
    dq, dk, dv = cross_bwd(q_cross, kv, frames, dattn, attn_cross, lse_cross, heads)
    g_one, do_kept, do_sent, sum_dq, sum_g_one, gain_two, shift_two = middle_back(core_at, dq, resid_one, g_two, w_mid, norm_gain)
    do_come = other(do_sent)
    d_kept, d_sent = self_bwd(core_at, kept, come, do_kept, do_come, o_kept, o_sent, lse_self,
                              seg_cont.reshape(-1, 1, BLK), seg_cont[:, None])
    d_kept, d_sent, output = lax.optimization_barrier((d_kept, d_sent, output))
    d_come = other(d_sent)
    dq_late, d_kept = lax.optimization_barrier((dq, d_kept))
    gw_mid, sum_dv = middle_weights(core_at, g_one, o_kept, o_come, norm_two, dq_late, mem, dk, dv, g_two, attn_cross)
    early = [gain_two, gain_three, shift_two, shift_three, sum_g_one, sum_dq, sum_dv, sum_g_two, sum_dpre, sum_g]
    if rows_here % 16 == 0:
        (g_qkv, g_attn_out, g_cross_q, g_cross_k, g_cross_v, g_cross_out, sums, g_mlp_in, g_mlp_out, grad_low) = end_all(
            gw_mid, d_kept, d_come, moved, norm_one, g_one, w_qkv, norm_gain, g_ff, early, chips)
    else:
        grad_low, gain_one, shift_one = qkv_back(core_at, d_kept, d_come, moved, g_one, w_qkv, norm_gain)
        grad_low = fix(grad_low)
        gw_qkv, sum_q, sum_v = qkv_weights(core_at, norm_one, d_kept, d_come)
        g_qkv, g_attn_out, g_cross_q, g_cross_k, g_cross_v, g_cross_out, sums, g_mlp_in, g_mlp_out = sum_all(
            jnp.concatenate([gw_qkv, gw_mid], 2), g_ff,
            [gain_one, *early[:2], shift_one, *early[2:4], sum_q, sum_v, *early[4:]], chips)
    grad_tokens = grad_low.astype(F32)
    g_gain, g_shift, g_proj = sums[:3], sums[3:6], sums[6:12]
    unit_rows = sum_dpre.shape[0]
    g_units, g_out_bias = sums[12:12 + unit_rows].reshape(-1), sums[12 + unit_rows]
    return (output, grad_tokens, g_qkv.transpose(1, 0, 2), g_attn_out.T, g_cross_q,
            jnp.stack([g_cross_k, g_cross_v], 1), g_cross_out.T, g_mlp_in, g_mlp_out.T,
            g_gain, g_shift, g_proj, g_units, g_out_bias)


def solution(mesh):
    grid = Mesh(mesh.devices.reshape(-1, 2, mesh.shape["tensor"]), ("chip", "core", "tensor"))
    rows = ("chip", "core", "tensor")
    dp = ("chip", "core")
    in_specs = (P(rows, None), P(dp, None, None), P(rows), P(rows), P(rows, None), P(dp, None, "tensor"), P("tensor", dp),
                P(dp, "tensor"), P(dp, None, "tensor"), P("tensor", dp), P(dp, "tensor"), P("tensor", dp),
                P(), P(), P(), P(), P())
    out_specs = (P(rows, None), P(rows, None), P(dp, None, "tensor"), P("tensor", dp), P(dp, "tensor"), P(dp, None, "tensor"),
                 P("tensor", dp), P(dp, "tensor"), P("tensor", dp), P(), P(), P(), P(), P())
    return jax.shard_map(on_device, mesh=grid, in_specs=in_specs, out_specs=out_specs, check_vma=False)
```

profile of v0, /device:TPU:0, one launch (start us, length us, event | category | flops | bytes accessed | tf_op | source)
XLA Modules:
  0.0 480.4 jit_solution(6947133079990787169)
XLA Ops:
  7.2 1.0 copy.34
  8.2 1.5 pad_maximum_fusion.1
  9.8 54.6 %gather_all.1 = (bf16[2,2,2,2,2,48,1152]{6,5,4,3,2,1,0:T(8,128)(2,1)}, s32[8,128]{1,0:T(8,128)}, bf16[1024,768]{1,0:T(8,128)(2,1)}) custom-call(bf16[3,48,384]{2,1,0:T(8,128)(2,1)} %bitcast.43, s32[8,128]{1,0:T(8,128)} %bitcast.53, bf16[1024,768]{1,0:T(8,128)(2,1)} %x_ref.1), custom_call_target="tpu_custom_call" | custom-call | bytes 1000000 | tf_op jit(solution)/shard_map/gather_all/pallas_call | solution.py:755
  65.3 1.3 slice.18
  66.6 7.0 %qkv_sent.1 = (bf16[1024,768]{1,0:T(8,128)(2,1)}, bf16[3,1024,384]{2,1,0:T(8,128)(2,1)}) custom-call(s32[1]{0:T(128)} %bitcast.core_ref, bf16[1024,768]{1,0:T(8,128)(2,1)} %get-tuple-element.80.x_ref.x_hbm, bf16[2,768,1152]{2,1,0:T(8,128)(2,1)} %bitcast.34, f32[3,768]{1,0:T(4,128)} %gain_ref.9, f32[3,768]{1,0:T(4,128)} %shift_ref.5, f32[2,2,384]{2,1,0:T(2,128)} %bitcast.51), custom_call_target="tpu_custom_call" | custom-call | flops 1811939328 | bytes 9830400 | tf_op jit(solution)/shard_map/qkv_sent/pallas_call | solution.py:342
  74.1 1.9 collective-permute-start.3
  76.0 1.0 copy.31.segq_ref.segk_ref
  77.0 6.3 %qkv_kept.1.kept_ref = bf16[3,1024,384]{2,1,0:T(8,128)(2,1)} custom-call(s32[1]{0:T(128)} %bitcast.core_ref, bf16[1024,768]{1,0:T(8,128)(2,1)} %get-tuple-element.83.norm_ref.norm_hbm, bf16[2,768,1152]{2,1,0:T(8,128)(2,1)} %bitcast.35, f32[2,2,384]{2,1,0:T(2,128)} %bitcast.52), custom_call_target="tpu_custom_call" | custom-call | flops 1811939328 | bytes 8257536 | tf_op jit(solution)/shard_map/qkv_kept/pallas_call | solution.py:355
  83.3 1.4 copy-done.14
  84.7 26.2 %self_fwd.1 = (bf16[1024,384]{1,0:T(8,128)(2,1)}, bf16[1024,384]{1,0:T(8,128)(2,1)}, f32[2048,384]{1,0:T(8,128)}) custom-call(s32[1]{0:T(128)} %bitcast.core_ref, bf16[3,1024,384]{2,1,0:T(8,128)(2,1)} %qkv_kept.1.kept_ref, bf16[3,1024,384]{2,1,0:T(8,128)(2,1)} %copy-done.14, s32[1024,1]{1,0:T(8,128)} %copy.31.segq_ref.segk_ref, s32[1,1024]{1,0:T(1,128)} %bitcast.54), custom_call_target="tpu_custom_call" | custom-call | flops 1811939328 | bytes 1179648 | tf_op jit(solution)/shard_map/self_fwd/pallas_call | solution.py:86
  111.0 2.0 collective-permute-start.2
  113.5 9.2 %memory_project.1 = (bf16[1536,1536]{1,0:T(8,128)(2,1)}, bf16[1536,768]{1,0:T(8,128)(2,1)}) custom-call(s32[1]{0:T(128)} %bitcast.10.mine_ref, bf16[1500,768]{1,0:T(8,128)(2,1)} %bitcast.60, bf16[1500,768]{1,0:T(8,128)(2,1)} %collective-permute-done.1.come_ref, bf16[2,768,1920]{2,1,0:T(8,128)(2,1)} %bitcast.28, f32[6,768]{1,0:T(8,128)} %bias_ref.5), custom_call_target="tpu_custom_call" | custom-call | flops 3538944000 | bytes 13879296 | tf_op jit(solution)/shard_map/memory_project/pallas_call | solution.py:380
  123.6 9.3 %middle.1 = (f32[1024,768]{1,0:T(8,128)}, bf16[1024,768]{1,0:T(8,128)(2,1)}, bf16[1024,768]{1,0:T(8,128)(2,1)}) custom-call(s32[1]{0:T(128)} %bitcast.core_ref, bf16[1024,768]{1,0:T(8,128)(2,1)} %get-tuple-element.80.x_ref.x_hbm, bf16[1024,384]{1,0:T(8,128)(2,1)} %get-tuple-element.86.own_ref.o_ref, bf16[1024,384]{1,0:T(8,128)(2,1)} %copy-done.3, ...), custom_call_target="tpu_custom_call" | custom-call | flops 2415919104 | bytes 11796480 | tf_op jit(solution)/shard_map/middle/pallas_call | solution.py:409
  132.9 27.5 %cross_fwd.1 = (bf16[1024,768]{1,0:T(8,128)(2,1)}, f32[1024,768]{1,0:T(8,128)}) custom-call(bf16[1024,768]{1,0:T(8,128)(2,1)} %get-tuple-element.91.q_ref, bf16[1536,1536]{1,0:T(8,128)(2,1)} %get-tuple-element.92.k_ref.v_ref, bf16[1536,1536]{1,0:T(8,128)(2,1)} %get-tuple-element.92.k_ref.v_ref), custom_call_target="tpu_custom_call" | custom-call | flops 2415919104 | bytes 1376256 | tf_op jit(solution)/shard_map/cross_fwd/pallas_call | solution.py:129
  160.4 11.7 %all-gather.5.cloned.1.call-done = bf16[1536,3072]{1,0:T(8,128)(2,1)} async-done(((bf16[48,3072]{1,0:T(8,128)(2,1)}), bf16[1536,3072]{1,0:T(8,128)(2,1)}) %all-gather.5.cloned.1.call-update) | async-done | bytes 9437200 | tf_op jit(solution)/shard_map/all_gather | solution.py:1052
  172.1 36.7 %feed.1 = (bf16[1024,768]{1,0:T(8,128)(2,1)}, bf16[1024,768]{1,0:T(8,128)(2,1)}, bf16[1024,3072]{1,0:T(8,128)(2,1)}, bf16[1024,3072]{1,0:T(8,128)(2,1)}, f32[102...) custom-call(s32[1]{0:T(128)} %bitcast.10.mine_ref, ...), custom_call_target="tpu_custom_call" | custom-call | flops 21743271936 | bytes 35782656 | tf_op jit(solution)/shard_map/feed/pallas_call | solution.py:491
  208.8 24.2 %feed_weights.1 = bf16[2,768,3072]{2,1,0:T(8,128)(2,1)} custom-call(bf16[1024,768]{1,0:T(8,128)(2,1)} %get-tuple-element.98.norm_ref, bf16[1024,768]{1,0:T(8,128)(2,1)} %get-tuple-element.99.g_ref, bf16[1024,3072]{1,0:T(8,128)(2,1)} %get-tuple-element.100.dpre_ref, bf16[1024,3072]{1,0:T(8,128)(2,1)} %get-tuple-element.101.hidden_ref), custom_call_target="tpu_custom_call" | custom-call | flops 9663676416 | bytes 22020096 | tf_op jit(solution)/shard_map/feed_weights/pallas_call | solution.py:514
  233.0 1.4 copy-done.15
  235.1 56.1 %cross_bwd.1 = (bf16[1024,768]{1,0:T(8,128)(2,1)}, bf16[1536,768]{1,0:T(8,128)(2,1)}, bf16[1536,768]{1,0:T(8,128)(2,1)}) custom-call(bf16[1024,768]{1,0:T(8,128)(2,1)} %get-tuple-element.91.q_ref, bf16[1536,1536]{1,0:T(8,128)(2,1)} %get-tuple-element.92.k_ref.v_ref, bf16[1536,1536]{1,0:T(8,128)(2,1)} %get-tuple-element.92.k_ref.v_ref, ...), custom_call_target="tpu_custom_call" | custom-call | flops 6039797760 | bytes 2359296 | tf_op jit(solution)/shard_map/cross_bwd/pallas_call | solution.py:263
  291.2 9.8 %middle_back.1 = (f32[1024,768]{1,0:T(8,128)}, bf16[1024,384]{1,0:T(8,128)(2,1)}, bf16[1024,384]{1,0:T(8,128)(2,1)}, f32[1,768]{1,0:T(1,128)}, f32[1,768]{1,0:T(...) custom-call(s32[1]{0:T(128)} %bitcast.core_ref, bf16[1024,768]{1,0:T(8,128)(2,1)} %get-tuple-element.116.dq_ref, ...), custom_call_target="tpu_custom_call" | custom-call | flops 2415919104 | bytes 16515072 | tf_op jit(solution)/shard_map/middle_back/pallas_call | solution.py:548
  301.0 2.8 collective-permute-start.4
  303.8 2.1 collective-permute-done.4.do_come_ref
  306.8 50.5 %self_bwd.1 = (bf16[3,1024,384]{2,1,0:T(8,128)(2,1)}, bf16[3,1024,384]{2,1,0:T(8,128)(2,1)}) custom-call(s32[1]{0:T(128)} %bitcast.core_ref, bf16[3,1024,384]{2,1,0:T(8,128)(2,1)} %qkv_kept.1.kept_ref, bf16[3,1024,384]{2,1,0:T(8,128)(2,1)} %copy-done.14, bf16[1024,384]{1,0:T(8,128)(2,1)} %get-tuple-element.106.do_ref, bf16[1024,384]{1,0:T(8,128)(2,1)} %copy-done.16, ...), custom_call_target="tpu_custom_call" | custom-call | flops 4529848320 | bytes 1966080 | tf_op jit(solution)/shard_map/self_bwd/pallas_call | solution.py:226
  357.4 1.1 copy-done.1
  359.0 17.8 %middle_weights.1 = (bf16[2,768,1920]{2,1,0:T(8,128)(2,1)}, f32[1,768]{1,0:T(1,128)}) custom-call(s32[1]{0:T(128)} %bitcast.core_ref, f32[1024,768]{1,0:T(8,128)} %get-tuple-element.113.g1_ref.g1_hbm, bf16[1024,384]{1,0:T(8,128)(2,1)} %get-tuple-element.86.own_ref.o_ref, bf16[1024,384]{1,0:T(8,128)(2,1)} %copy-done.3, ...), custom_call_target="tpu_custom_call" | custom-call | flops 7247757312 | bytes 28704768 | tf_op jit(solution)/shard_map/middle_weights/pallas_call | solution.py:576
  376.8 1.4 copy-done
  378.2 79.6 %end_all.1 = (f32[3,48,384]{2,1,0:T(8,128)}, f32[48,384]{1,0:T(8,128)}, f32[48,384]{1,0:T(8,128)}, f32[48,384]{1,0:T(8,128)}, f32[48,384]{1,0:T(8,128)}, /*index...) custom-call(bf16[2,2,2,2,2,48,1920]{6,5,4,3,2,1,0:T(8,128)(2,1)} %bi, ...), custom_call_target="tpu_custom_call" | custom-call | bytes 1000000 | tf_op jit(solution)/shard_map/end_all/pallas_call | solution.py:1034
  457.8 1.3 slice_reduce_fusion
  459.9 1.4 slice.21
  461.3 1.4 fusion
  465.0 3.4 convert_element_type.4
  468.5 1.1 copy.42
  (60 shorter events, 12.1 us)
Async XLA Ops:
  7.2 57.3 %copy-start.7 = (bf16[1536,48]{0,1:T(8,128)(2,1)S(1)}, bf16[1536,48]{0,1:T(8,128)(2,1)}, u32[]{:S(2)}) copy-start(bf16[1536,48]{0,1:T(8,128)(2,1)} %param.27) | copy-start | bytes 442372
  7.2 57.3 %copy-start.8 = (bf16[48,1536]{1,0:T(8,128)(2,1)S(1)}, bf16[48,1536]{1,0:T(8,128)(2,1)}, u32[]{:S(2)}) copy-start(bf16[48,1536]{1,0:T(8,128)(2,1)} %param.26) | copy-start | bytes 442372
  7.2 106.3 %all-gather.3.cloned.1.call-start = ((), (), s32[]{:S(2)}) async-start(), calls=%async_computation.1 | async-start | bytes 6082560 | tf_op jit(solution)/shard_map/all_gather | solution.py:1052
  9.7 162.4 %all-gather.5.cloned.1.call-start = ((), (), s32[]{:S(2)}) async-start(), calls=%async_computation.2 | async-start | bytes 9732096 | tf_op jit(solution)/shard_map/all_gather | solution.py:1052
  65.2 311.6 %reduce-scatter.2.cloned.1.call-start = ((), (), s32[]{:S(2)}) async-start(), calls=%async_computation.3 | async-start | bytes 9732096 | tf_op jit(solution)/shard_map/reduce_scatter | solution.py:1057
  66.6 9.4 %copy-start.12 = (s32[8,128]{1,0:T(8,128)S(1)}, s32[8,128]{1,0:T(8,128)}, u32[]{:S(2)}) copy-start(s32[8,128]{1,0:T(8,128)} %get-tuple-element.85) | copy-start | bytes 12292
  73.6 9.7 %collective-permute-start = (bf16[3,1024,384]{2,1,0:T(8,128)(2,1)}, bf16[3,1024,384]{2,1,0:T(8,128)(2,1)S(1)}, u32[]{:S(2)}, u32[]{:S(2)}) collective-permute-start(bf16[3,1024,384]{2,1,0:T(8,128)(2,1)} %get-tuple-element.84), channel_id=1, source_target_pairs={{0,2},{2,0},{1,3},{3,1},{4,6},{6,4},{5,7},{7,5},{8,10},{10,8},{9,1... | collective-permute-start | bytes 7077896 | tf_op jit(solution)/shard_map/ppermute | solution.py:1073
  73.9 39.5 %collective-permute-start.1 = (bf16[1500,768]{1,0:T(8,128)(2,1)}, bf16[1500,768]{1,0:T(8,128)(2,1)}, u32[]{:S(2)}, u32[]{:S(2)}) collective-permute-start(bf16[1500,768]{1,0:T(8,128)(2,1)} %bitcast.59), channel_id=1, source_target_pairs={{0,2},{2,0},{1,3},{3,1},{4,6},{6,4},{5,7},{7,5},{8,10},{10,8},{9,1... | collective-permute-start | bytes 6912008 | tf_op jit(solution)/shard_map/ppermute | solution.py:1073
  74.1 86.3 %collective-permute-start.3 = (bf16[1024,768]{1,0:T(8,128)(2,1)}, bf16[1024,768]{1,0:T(8,128)(2,1)}, u32[]{:S(2)}, u32[]{:S(2)}) collective-permute-start(bf16[1024,768]{1,0:T(8,128)(2,1)} %g_own_ref.1), channel_id=1, source_target_pairs={{1,2},{2,1},{5,6},{6,5},{9,10},{10,9},{13,14},{14,13},{17,18},{18,... | collective-permute-start | bytes 4718600 | tf_op jit(solution)/shard_map/ppermute | solution.py:1087
  83.3 1.4 copy-start.14
  84.7 28.2 %copy-start.13 = (f32[768]{0:T(1024)S(1)}, f32[768]{0:T(1024)}, u32[]{:S(2)}) copy-start(f32[768]{0:T(1024)} %param.32) | copy-start | bytes 9220
  111.0 11.7 %collective-permute-start.2 = (bf16[1024,384]{1,0:T(8,128)(2,1)}, bf16[1024,384]{1,0:T(8,128)(2,1)S(1)}, u32[]{:S(2)}, u32[]{:S(2)}) collective-permute-start(bf16[1024,384]{1,0:T(8,128)(2,1)} %get-tuple-element.89.o_sent_ref), channel_id=1, source_target_pairs={{0,2},{2,0},{1,3},{3,1},{4,6},{6,4},{5,7},{7,5},{8,10},{10,8},{9,1... | collective-permute-start | bytes 2359304 | tf_op jit(solution)/shard_map/ppermute | solution.py:1073
  122.7 0.9 copy-start.3
  232.9 1.4 copy-start.15
  234.3 123.0 %collective-permute-start.5 = (bf16[1024,768]{1,0:T(8,128)(2,1)S(1)}, bf16[1024,768]{1,0:T(8,128)(2,1)S(1)}, u32[]{:S(2)}, u32[]{:S(2)}) collective-permute-start(bf16[1024,768]{1,0:T(8,128)(2,1)S(1)} %copy-done.15), channel_id=1, source_target_pairs={{0,0},{1,2},{2,1},{3,3},{4,4},{5,6},{6,5},{7,7},{8,8},{9,10},{10,9... | collective-permute-start | bytes 4718600 | tf_op jit(solution)/shard_map/ppermute | solution.py:1072
  301.0 4.9 %collective-permute-start.4 = (bf16[1024,384]{1,0:T(8,128)(2,1)}, bf16[1024,384]{1,0:T(8,128)(2,1)S(1)}, u32[]{:S(2)}, u32[]{:S(2)}) collective-permute-start(bf16[1024,384]{1,0:T(8,128)(2,1)} %get-tuple-element.107), channel_id=1, source_target_pairs={{0,2},{2,0},{1,3},{3,1},{4,6},{6,4},{5,7},{7,5},{8,10},{10,8},{9,1... | collective-permute-start | bytes 2359304 | tf_op jit(solution)/shard_map/ppermute | solution.py:1073
  305.9 0.9 copy-start.16
  357.4 1.1 copy-start.1
  358.5 18.2 %collective-permute-start.6 = (bf16[3,1024,384]{2,1,0:T(8,128)(2,1)}, bf16[3,1024,384]{2,1,0:T(8,128)(2,1)S(1)}, u32[]{:S(2)}, u32[]{:S(2)}) collective-permute-start(bf16[3,1024,384]{2,1,0:T(8,128)(2,1)} %get-tuple-element.122), channel_id=1, source_target_pairs={{0,2},{2,0},{1,3},{3,1},{4,6},{6,4},{5,7},{7,5},{8,10},{10,8},{9,1... | collective-permute-start | bytes 7077896 | tf_op jit(solution)/shard_map/ppermute | solution.py:1073
  376.8 1.4 copy-start
  465.0 3.5 copy-start.2
  468.4 1.2 copy-start.6
  468.4 1.9 copy-start.11
  468.4 2.5 copy-start.10
  468.4 3.1 copy-start.9
  468.4 3.8 copy-start.5
  468.4 4.5 copy-start.4
Sparse Core Ops, SparseCore 0:
  11.5 75.9 all-gather.2
  91.0 81.0 all-gather.4
  233.1 134.2 reduce-scatter.1
where the time goes:
time: 485 us; the launch traced here: 480 us
  Pallas kernels  415 us (86%)
  local copies, waits for them, and re-layouts  22.5 us (5%)
  between operations  14.1 us (3%)
  waiting for transfers between devices  13.9 us (3%)
  starting transfers between devices  8.45 us (2%)
  other arithmetic  6.58 us (1%)
    pallas_call x1, Pallas kernels, end_all(): pl.pallas_call(functools.partial(end_kernel, names, orders, mid_lanes, qk...  79.6 us
    pallas_call x1, Pallas kernels, cross_bwd(): pl.pallas_call(functools.partial(cross_bwd_kernel, frames), grid=(npair,)...  56.1 us
    pallas_call x1, Pallas kernels, gather_all(): pl.pallas_call(functools.partial(gather_kernel, names, orders), in_specs=...  54.6 us
    pallas_call x1, Pallas kernels, self_bwd(): pl.pallas_call(self_bwd_kernel, grid=(part // LANES,), in_specs=[scalar()...  50.5 us
    pallas_call x1, Pallas kernels, feed(): pl.pallas_call(feed_kernel, grid=(rows // ROWS,), in_specs=[scalar(), by_...  36.7 us
    pallas_call x1, Pallas kernels, cross_fwd(): pl.pallas_call(functools.partial(cross_fwd_kernel, frames), grid=(npair,)...  27.5 us
    pallas_call x1, Pallas kernels, self_fwd(): pl.pallas_call(self_fwd_kernel, grid=(part // LANES,), in_specs=[scalar()...  26.2 us
    pallas_call x1, Pallas kernels, feed_weights(): pl.pallas_call(feed_weights_kernel, grid=(2, 2), in_specs=[whole(norm.sha...  24.2 us
  transfers between devices with their start and end apart: 10, of which 2 were waited for; matrix products, arithmetic and copies ran while one was open for 1% of the time, Pallas kernels for 57%

commit v1 on v0

--- a/solution.py
+++ b/solution.py
@@ -325,8 +325,10 @@
     out_ref[2] = (cols[:, 2 * part:] + bias_ref[at, 1:2]).astype(BF)
 
 
-def qkv_sent_kernel(core_ref, x_ref, w_ref, gain_ref, shift_ref, bias_ref, norm_ref, sent_ref):
-    normed, _ = normalize(x_ref[...].astype(F32))
+def qkv_sent_kernel(core_ref, mine_ref, x_own_ref, x_come_ref, w_ref, gain_ref, shift_ref, bias_ref, norm_ref, sent_ref, x_ref):
+    x = jnp.where(mine_ref[0] == 1, x_own_ref[...], x_come_ref[...])
+    x_ref[...] = x
+    normed, _ = normalize(x.astype(F32))
     low = (normed * gain_ref[0:1] + shift_ref[0:1]).astype(BF)
     norm_ref[...] = low
     qkv_heads(low, w_ref, bias_ref, 1 - core_ref[0], sent_ref)
@@ -336,17 +338,17 @@
     qkv_heads(norm_ref[...], w_ref, bias_ref, core_ref[0], kept_ref)
 
 
-def qkv_sent(core, x, w, gain, shift, bias):
-    rows, width = x.shape
+def qkv_sent(core, mine, x_own, x_come, w, gain, shift, bias):
+    rows, width = x_own.shape
     part = width // 2
     return pl.pallas_call(
         qkv_sent_kernel, grid=(rows // ROWS,),
-        in_specs=[scalar(), by_rows(width), whole(w.shape), whole(gain.shape), whole(shift.shape), whole(bias.shape)],
-        out_specs=[by_rows(width), by_rows(3, part)],
-        out_shape=[shaped((rows, width), BF), shaped((3, rows, part), BF)],
+        in_specs=[scalar(), scalar(), by_rows(width), by_rows(width), whole(w.shape), whole(gain.shape), whole(shift.shape), whole(bias.shape)],
+        out_specs=[by_rows(width), by_rows(3, part), by_rows(width)],
+        out_shape=[shaped((rows, width), BF), shaped((3, rows, part), BF), shaped((rows, width), BF)],
         compiler_params=pltpu.CompilerParams(vmem_limit_bytes=BIG),
         cost_estimate=cost(3 * rows * width * width, 2 * (3 * width * width + 4 * rows * width)), name="qkv_sent",
-    )(core, x, w, gain, shift, bias)
+    )(core, mine, x_own, x_come, w, gain, shift, bias)
 
 
 def qkv_kept(core, norm, w, bias):
@@ -675,22 +677,40 @@
     return [slice(a, b) for a, b in zip(cuts, cuts[1:])]
 
 
-def gather_kernel(names, orders, own_ref, seg_ref, x_ref, out_ref, seg_out_ref, moved_ref, block, segs, local_sem, send_sem, recv_sem):
+CHUNKS = 8
+
+
+class Swap:
+    def __init__(self, src_ref, dst_ref, send_sem, recv_sem):
+        core, tensor = lax.axis_index("core"), lax.axis_index("tensor")
+        cut = src_ref.shape[0] // CHUNKS
+        self.differ, self.started = core != tensor, 0
+        self.copies = [pltpu.make_async_remote_copy(
+            src_ref.at[i * cut:(i + 1) * cut], dst_ref.at[i * cut:(i + 1) * cut], send_sem.at[i], recv_sem.at[i],
+            device_id={"core": tensor, "tensor": core}, device_id_type=pl.DeviceIdType.MESH) for i in range(CHUNKS)]
+
+    def some(self, count):
+        chosen = self.copies[self.started:self.started + count]
+        self.started += len(chosen)
+        if chosen:
+            @pl.when(self.differ)
+            def _():
+                for copy in chosen:
+                    copy.start()
+
+    def wait(self):
+        @pl.when(self.differ)
+        def _():
+            for copy in self.copies:
+                copy.wait()
+
+
+def gather_kernel(names, orders, own_ref, seg_ref, x_ref, out_ref, seg_out_ref, moved_ref, block, segs, local_sem, send_sem, recv_sem,
+                  swap_send, swap_recv):
     core, tensor = lax.axis_index("core"), lax.axis_index("tensor")
     greet(names, {"core": 1 - core, "tensor": 1 - tensor})
     spare = len(orders)
-    swap = pltpu.make_async_remote_copy(x_ref, moved_ref, send_sem.at[spare, 2], recv_sem.at[spare, 2],
-                                        device_id={"core": tensor, "tensor": core}, device_id_type=pl.DeviceIdType.MESH)
-    stay = pltpu.make_async_copy(x_ref, moved_ref, local_sem.at[1])
-
-    @pl.when(core != tensor)
-    def _():
-        swap.start()
-
-    @pl.when(core == tensor)
-    def _():
-        stay.start()
-
+    swap = Swap(x_ref, moved_ref, swap_send, swap_recv)
     pieces, _, part = own_ref.shape
     for i in range(pieces):
         block[:, i * part:(i + 1) * part] = own_ref[i]
@@ -720,12 +740,14 @@
     local.start()
     segs[core, tensor] = seg_ref[...]
     along = send(segs.at[core, tensor], segs.at[core, tensor], spare, 0, "t")
+    swap.some(2)
     local.wait()
     for step in range(len(names)):
         for st in range(len(orders)):
             flying[st].wait_recv()
             if step + 1 < len(names):
                 start(st, step + 1)
+        swap.some(2)
         if step == 0:
             along.wait_recv()
             along = send(segs.at[core], segs.at[core], spare, 1, "core")
@@ -733,14 +755,7 @@
     seg_out_ref[...] = segs[tensor, 1]
     for copy in sent:
         copy.wait_send()
-
-    @pl.when(core != tensor)
-    def _():
-        swap.wait()
-
-    @pl.when(core == tensor)
-    def _():
-        stay.wait()
+    swap.wait()
 
 
 def gather_all(shard, seg, x, chips):
@@ -757,7 +772,8 @@
         in_specs=[vmem, vmem, hbm], out_specs=[hbm, vmem, hbm],
         out_shape=[shaped((2,) * len(names) + (rows, cols), shard.dtype), shaped(seg.shape, seg.dtype), shaped(x.shape, x.dtype)],
         scratch_shapes=[pltpu.VMEM((rows, cols), shard.dtype), pltpu.VMEM((2, 2) + seg.shape, seg.dtype),
-                        dma((2,)), dma((len(orders) + 1, len(names))), dma((len(orders) + 1, len(names)))],
+                        dma((2,)), dma((len(orders) + 1, len(names))), dma((len(orders) + 1, len(names))),
+                        dma((CHUNKS,)), dma((CHUNKS,))],
         compiler_params=pltpu.CompilerParams(collective_id=0, has_side_effects=True, vmem_limit_bytes=BIG),
         cost_estimate=cost(0, 1e6), name="gather_all",
     )(shard, seg, x)
@@ -922,7 +938,7 @@
     parts = mid_hbm.shape[-1] // qkv_ref.shape[2]
     mid_refs, refs = refs[:parts], refs[parts:]
     (small_out_ref, ff_in_ref, ff_out_ref, moved_ref, mid, kept, come, x, norm, g1, w, grad_qkv, grad_low, small_first, small_recv,
-     small_held, load_sem, send_sem, recv_sem, *bufs) = refs
+     small_held, load_sem, send_sem, recv_sem, swap_send, swap_recv, *bufs) = refs
     core, tensor = lax.axis_index("core"), lax.axis_index("tensor")
     steps = len(names)
     part = qkv_ref.shape[2]
@@ -969,14 +985,9 @@
         if b == 1:
             loads[0].wait()
             step_mid()
-    spare = len(sums.streams) + len(qkv_lanes) + 1
-    swap = pltpu.make_async_remote_copy(grad_low, moved_ref, send_sem.at[spare, 0], recv_sem.at[spare, 0],
-                                        device_id={"core": tensor, "tensor": core}, device_id_type=pl.DeviceIdType.MESH)
+    swap = Swap(grad_low, moved_ref, swap_send, swap_recv)
     stay = pltpu.make_async_copy(grad_low, moved_ref, load_sem.at[7])
-
-    @pl.when(core != tensor)
-    def _():
-        swap.start()
+    swap.some(CHUNKS)
 
     @pl.when(core == tensor)
     def _():
@@ -991,6 +1002,7 @@
             grad_qkv[(t,) + everything[1:] + (slice(j * part, (j + 1) * part),)] = grad.reshape(grad_qkv.shape[1:-1] + (part,))
             bias.append(column_sum(ref[j].astype(F32)))
         step_mid()
+        swap.some(2)
     for lane, order, (recv, held) in zip(qkv_lanes, orders, split_bufs(bufs[split:], steps, len(qkv_lanes))):
         ref = grad_qkv.at[everything + (lane,)]
         sums.start(sums.add(ref, ref, order, recv, held, put_pieces(lane, part, qkv_place)))
@@ -1003,11 +1015,9 @@
     sums.start(sums.add(small_first, None, orders[0], [small_recv.at[i] for i in range(steps)],
                         [small_held.at[i] for i in range(steps - 1)], small_out))
     unpack_ff(ff_ref, ff_in_ref, ff_out_ref)
+    swap.some(CHUNKS)
     sums.finish()
-
-    @pl.when(core != tensor)
-    def _():
-        swap.wait()
+    swap.wait()
 
     @pl.when(core == tensor)
     def _():
@@ -1038,7 +1048,7 @@
         + [shaped(shape, F32)] + [shaped((here, ff.shape[1] // 2), F32)] * 2 + [shaped((rows, width), BF)],
         scratch_shapes=[pltpu.VMEM(v.shape, v.dtype) for v in (mid, kept, come, x, norm, g1, w)]
         + [pltpu.VMEM(lead + (here, 3 * part), BF), pltpu.VMEM((rows, width), BF)] + extra
-        + [dma((8,)), dma((count, steps)), dma((count, steps))]
+        + [dma((8,)), dma((count, steps)), dma((count, steps)), dma((CHUNKS,)), dma((CHUNKS,))]
         + sum_bufs(steps, here, mid_lanes) + sum_bufs(steps, here, qkv_lanes),
         compiler_params=pltpu.CompilerParams(collective_id=1, has_side_effects=True, vmem_limit_bytes=BIG),
         cost_estimate=cost(0, 1e6), name="end_all",
@@ -1076,12 +1086,12 @@
     mid = jnp.concatenate([attn_out.T, cross_q, cross_kv.reshape(rows_here, 2 * part), cross_out.T], 1)
     first, mid = lax.optimization_barrier((attn_in.transpose(1, 0, 2), mid))
     w_mid = fetch(mid)
-    w_qkv, seg_cont, moved = gather_all(first, seg_ids, tokens, chips)
+    w_qkv, seg_cont, x_come = gather_all(first, seg_ids, tokens, chips)
     late_in, late_out, w_qkv = lax.optimization_barrier((mlp_in, mlp_out, w_qkv))
     w_ff = fetch(jnp.concatenate([late_in, late_out.T], 1))
     bias_halves = proj_bias[:2].reshape(2, 2, part).transpose(1, 0, 2)
 
-    norm_one, sent = qkv_sent(core_at, moved, w_qkv, norm_gain, norm_bias, bias_halves)
+    norm_one, sent, moved = qkv_sent(core_at, mine, tokens, x_come, w_qkv, norm_gain, norm_bias, bias_halves)
     come = other(sent)
     kept = qkv_kept(core_at, norm_one, w_qkv, bias_halves)
     grad_come = lax.ppermute(grad_output, ("core", "tensor"), [(1, 2), (2, 1)])

time: 485 us -> 483 us (level); the launches traced: 480 us -> 473 us
  Pallas kernels: 415 us -> 387 us
  waiting for transfers between devices: 13.9 us -> 35.4 us
    all_gather x2, waiting for transfers between devices: 11.7 us -> 33.2 us  [fetch(): full = lax.all_gather(shard, ALL, axis=0, tiled=True)]
    pallas_call x1, Pallas kernels: 54.6 us -> 35.2 us  [gather_all(): pl.pallas_call(functools.partial(gather_kernel, names, orders), in_specs=...]
    pallas_call x1, Pallas kernels: 24.2 us -> 15.3 us  [feed_weights(): pl.pallas_call(feed_weights_kernel, grid=(2, 2), in_specs=[whole(norm.sha...]
  transfers between devices with their start and end apart: 10 -> 10, of which waited for: 2 -> 2; matrix products, arithmetic and copies ran while one was open for 1% -> 1% of each run, Pallas kernels for 57% -> 54%
where the time goes in v1:
time: 483 us; the launch traced here: 473 us
  Pallas kernels  387 us (80%)
  waiting for transfers between devices  35.4 us (7%)
  local copies, waits for them, and re-layouts  22.5 us (5%)
  between operations  14.2 us (3%)
  starting transfers between devices  7.56 us (2%)
  other arithmetic  6.58 us (1%)
    pallas_call x1, Pallas kernels, end_all(): pl.pallas_call(functools.partial(end_kernel, names, orders, mid_lanes, qk...  79.7 us
    pallas_call x1, Pallas kernels, cross_bwd(): pl.pallas_call(functools.partial(cross_bwd_kernel, frames), grid=(npair,)...  56.1 us
    pallas_call x1, Pallas kernels, self_bwd(): pl.pallas_call(self_bwd_kernel, grid=(part // LANES,), in_specs=[scalar()...  50.5 us
    pallas_call x1, Pallas kernels, feed(): pl.pallas_call(feed_kernel, grid=(rows // ROWS,), in_specs=[scalar(), by_...  36.7 us
    pallas_call x1, Pallas kernels, gather_all(): pl.pallas_call(functools.partial(gather_kernel, names, orders), in_specs=...  35.2 us
    all_gather x2, waiting for transfers between devices, fetch(): full = lax.all_gather(shard, ALL, axis=0, tiled=True)  33.2 us
    pallas_call x1, Pallas kernels, cross_fwd(): pl.pallas_call(functools.partial(cross_fwd_kernel, frames), grid=(npair,)...  27.6 us
    pallas_call x1, Pallas kernels, self_fwd(): pl.pallas_call(self_fwd_kernel, grid=(part // LANES,), in_specs=[scalar()...  26.1 us
  transfers between devices with their start and end apart: 10, of which 2 were waited for; matrix products, arithmetic and copies ran while one was open for 1% of the time, Pallas kernels for 54%

profile of v1, /device:TPU:0, one launch (start us, length us, event | category | flops | bytes accessed | tf_op | source)
XLA Modules:
  0.0 473.5 jit_solution(5263315678697482025)
XLA Ops:
  7.2 1.0 copy.34
  8.2 1.5 pad_maximum_fusion.1
  9.8 35.2 %gather_all.1 = (bf16[2,2,2,2,2,48,1152]{6,5,4,3,2,1,0:T(8,128)(2,1)}, s32[8,128]{1,0:T(8,128)}, bf16[1024,768]{1,0:T(8,128)(2,1)}) custom-call(bf16[3,48,384]{2,1,0:T(8,128)(2,1)} %bitcast.43, s32[8,128]{1,0:T(8,128)} %bitcast.53, bf16[1024,768]{1,0:T(8,128)(2,1)} %x_own_ref.1), custom_call_target="tpu_custom_call" | custom-call | bytes 1000000 | tf_op jit(solution)/shard_map/gather_all/pallas_call | solution.py:770
  45.8 1.3 slice.18
  47.1 7.6 %qkv_sent.1 = (bf16[1024,768]{1,0:T(8,128)(2,1)}, bf16[3,1024,384]{2,1,0:T(8,128)(2,1)}, bf16[1024,768]{1,0:T(8,128)(2,1)}) custom-call(s32[1]{0:T(128)} %bitcast.core_ref, s32[1]{0:T(128)} %bitcast.1.mine_ref, bf16[1024,768]{1,0:T(8,128)(2,1)} %x_own_ref.1, bf16[1024,768]{1,0:T(8,128)(2,1)} %get-tuple-element.81.x_come_ref, bf16[2,768,1152]{2,1,0:T(8,128)(2,1)} %bitcast.34, ...), custom_call_target="tpu_custom_call" | custom-call | flops 1811939328 | bytes 9830400 | tf_op jit(solution)/shard_map/qkv_sent/pallas_call | solution.py:344
  54.8 1.0 collective-permute-start
  55.9 1.9 collective-permute-start.3
  57.8 1.0 copy.31.segq_ref.segk_ref
  58.8 6.3 %qkv_kept.1.kept_ref = bf16[3,1024,384]{2,1,0:T(8,128)(2,1)} custom-call(s32[1]{0:T(128)} %bitcast.core_ref, bf16[1024,768]{1,0:T(8,128)(2,1)} %get-tuple-element.84.norm_ref.norm_hbm, bf16[2,768,1152]{2,1,0:T(8,128)(2,1)} %bitcast.35, f32[2,2,384]{2,1,0:T(2,128)} %bitcast.50), custom_call_target="tpu_custom_call" | custom-call | flops 1811939328 | bytes 8257536 | tf_op jit(solution)/shard_map/qkv_kept/pallas_call | solution.py:357
  65.1 1.4 copy-done.14
  66.5 26.1 %self_fwd.1 = (bf16[1024,384]{1,0:T(8,128)(2,1)}, bf16[1024,384]{1,0:T(8,128)(2,1)}, f32[2048,384]{1,0:T(8,128)}) custom-call(s32[1]{0:T(128)} %bitcast.core_ref, bf16[3,1024,384]{2,1,0:T(8,128)(2,1)} %qkv_kept.1.kept_ref, bf16[3,1024,384]{2,1,0:T(8,128)(2,1)} %copy-done.14, s32[1024,1]{1,0:T(8,128)} %copy.31.segq_ref.segk_ref, s32[1,1024]{1,0:T(1,128)} %bitcast.54), custom_call_target="tpu_custom_call" | custom-call | flops 1811939328 | bytes 1179648 | tf_op jit(solution)/shard_map/self_fwd/pallas_call | solution.py:86
  93.7 9.2 %memory_project.1 = (bf16[1536,1536]{1,0:T(8,128)(2,1)}, bf16[1536,768]{1,0:T(8,128)(2,1)}) custom-call(s32[1]{0:T(128)} %bitcast.1.mine_ref, bf16[1500,768]{1,0:T(8,128)(2,1)} %bitcast.60, bf16[1500,768]{1,0:T(8,128)(2,1)} %collective-permute-done.1.come_ref, bf16[2,768,1920]{2,1,0:T(8,128)(2,1)} %bitcast.28, f32[6,768]{1,0:T(8,128)} %bias_ref.5), custom_call_target="tpu_custom_call" | custom-call | flops 3538944000 | bytes 13879296 | tf_op jit(solution)/shard_map/memory_project/pallas_call | solution.py:382
  103.8 9.3 %middle.1 = (f32[1024,768]{1,0:T(8,128)}, bf16[1024,768]{1,0:T(8,128)(2,1)}, bf16[1024,768]{1,0:T(8,128)(2,1)}) custom-call(s32[1]{0:T(128)} %bitcast.core_ref, bf16[1024,768]{1,0:T(8,128)(2,1)} %get-tuple-element.86.x_ref.x_hbm, bf16[1024,384]{1,0:T(8,128)(2,1)} %get-tuple-element.88.own_ref.o_ref, bf16[1024,384]{1,0:T(8,128)(2,1)} %copy-done.3, ...), custom_call_target="tpu_custom_call" | custom-call | flops 2415919104 | bytes 11796480 | tf_op jit(solution)/shard_map/middle/pallas_call | solution.py:411
  113.1 27.6 %cross_fwd.1 = (bf16[1024,768]{1,0:T(8,128)(2,1)}, f32[1024,768]{1,0:T(8,128)}) custom-call(bf16[1024,768]{1,0:T(8,128)(2,1)} %get-tuple-element.93.q_ref, bf16[1536,1536]{1,0:T(8,128)(2,1)} %get-tuple-element.94.k_ref.v_ref, bf16[1536,1536]{1,0:T(8,128)(2,1)} %get-tuple-element.94.k_ref.v_ref), custom_call_target="tpu_custom_call" | custom-call | flops 2415919104 | bytes 1376256 | tf_op jit(solution)/shard_map/cross_fwd/pallas_call | solution.py:129
  140.7 33.2 %all-gather.5.cloned.1.call-done = bf16[1536,3072]{1,0:T(8,128)(2,1)} async-done(((bf16[48,3072]{1,0:T(8,128)(2,1)}), bf16[1536,3072]{1,0:T(8,128)(2,1)}) %all-gather.5.cloned.1.call-update) | async-done | bytes 9437200 | tf_op jit(solution)/shard_map/all_gather | solution.py:1062
  173.9 36.7 %feed.1 = (bf16[1024,768]{1,0:T(8,128)(2,1)}, bf16[1024,768]{1,0:T(8,128)(2,1)}, bf16[1024,3072]{1,0:T(8,128)(2,1)}, bf16[1024,3072]{1,0:T(8,128)(2,1)}, f32[102...) custom-call(s32[1]{0:T(128)} %bitcast.1.mine_ref, ...), custom_call_target="tpu_custom_call" | custom-call | flops 21743271936 | bytes 35782656 | tf_op jit(solution)/shard_map/feed/pallas_call | solution.py:493
  210.6 15.3 %feed_weights.1 = bf16[2,768,3072]{2,1,0:T(8,128)(2,1)} custom-call(bf16[1024,768]{1,0:T(8,128)(2,1)} %get-tuple-element.100.norm_ref, bf16[1024,768]{1,0:T(8,128)(2,1)} %get-tuple-element.101.g_ref, bf16[1024,3072]{1,0:T(8,128)(2,1)} %get-tuple-element.102.dpre_ref, bf16[1024,3072]{1,0:T(8,128)(2,1)} %get-tuple-element.103.hidden_ref), custom_call_target="tpu_custom_call" | custom-call | flops 9663676416 | bytes 22020096 | tf_op jit(solution)/shard_map/feed_weights/pallas_call | solution.py:516
  225.9 1.4 copy-done.15
  228.1 56.1 %cross_bwd.1 = (bf16[1024,768]{1,0:T(8,128)(2,1)}, bf16[1536,768]{1,0:T(8,128)(2,1)}, bf16[1536,768]{1,0:T(8,128)(2,1)}) custom-call(bf16[1024,768]{1,0:T(8,128)(2,1)} %get-tuple-element.93.q_ref, bf16[1536,1536]{1,0:T(8,128)(2,1)} %get-tuple-element.94.k_ref.v_ref, bf16[1536,1536]{1,0:T(8,128)(2,1)} %get-tuple-element.94.k_ref.v_ref, ...), custom_call_target="tpu_custom_call" | custom-call | flops 6039797760 | bytes 2359296 | tf_op jit(solution)/shard_map/cross_bwd/pallas_call | solution.py:263
  284.1 9.8 %middle_back.1 = (f32[1024,768]{1,0:T(8,128)}, bf16[1024,384]{1,0:T(8,128)(2,1)}, bf16[1024,384]{1,0:T(8,128)(2,1)}, f32[1,768]{1,0:T(1,128)}, f32[1,768]{1,0:T(...) custom-call(s32[1]{0:T(128)} %bitcast.core_ref, bf16[1024,768]{1,0:T(8,128)(2,1)} %get-tuple-element.118.dq_ref, ...), custom_call_target="tpu_custom_call" | custom-call | flops 2415919104 | bytes 16515072 | tf_op jit(solution)/shard_map/middle_back/pallas_call | solution.py:550
  293.9 2.8 collective-permute-start.4
  296.7 2.1 collective-permute-done.4.do_come_ref
  299.8 50.5 %self_bwd.1 = (bf16[3,1024,384]{2,1,0:T(8,128)(2,1)}, bf16[3,1024,384]{2,1,0:T(8,128)(2,1)}) custom-call(s32[1]{0:T(128)} %bitcast.core_ref, bf16[3,1024,384]{2,1,0:T(8,128)(2,1)} %qkv_kept.1.kept_ref, bf16[3,1024,384]{2,1,0:T(8,128)(2,1)} %copy-done.14, bf16[1024,384]{1,0:T(8,128)(2,1)} %get-tuple-element.108.do_ref, bf16[1024,384]{1,0:T(8,128)(2,1)} %copy-done.16, ...), custom_call_target="tpu_custom_call" | custom-call | flops 4529848320 | bytes 1966080 | tf_op jit(solution)/shard_map/self_bwd/pallas_call | solution.py:226
  350.3 1.1 copy-done.1
  351.9 17.8 %middle_weights.1 = (bf16[2,768,1920]{2,1,0:T(8,128)(2,1)}, f32[1,768]{1,0:T(1,128)}) custom-call(s32[1]{0:T(128)} %bitcast.core_ref, f32[1024,768]{1,0:T(8,128)} %get-tuple-element.115.g1_ref.g1_hbm, bf16[1024,384]{1,0:T(8,128)(2,1)} %get-tuple-element.88.own_ref.o_ref, bf16[1024,384]{1,0:T(8,128)(2,1)} %copy-done.3, ...), custom_call_target="tpu_custom_call" | custom-call | flops 7247757312 | bytes 28704768 | tf_op jit(solution)/shard_map/middle_weights/pallas_call | solution.py:578
  369.8 1.4 copy-done
  371.1 79.7 %end_all.1 = (f32[3,48,384]{2,1,0:T(8,128)}, f32[48,384]{1,0:T(8,128)}, f32[48,384]{1,0:T(8,128)}, f32[48,384]{1,0:T(8,128)}, f32[48,384]{1,0:T(8,128)}, /*index...) custom-call(bf16[2,2,2,2,2,48,1920]{6,5,4,3,2,1,0:T(8,128)(2,1)} %bi, ...), custom_call_target="tpu_custom_call" | custom-call | bytes 1000000 | tf_op jit(solution)/shard_map/end_all/pallas_call | solution.py:1044
  450.9 1.3 slice_reduce_fusion
  453.0 1.4 slice.21
  454.4 1.4 fusion
  458.1 3.4 convert_element_type.4
  461.5 1.1 copy.42
  (60 shorter events, 12.2 us)
Async XLA Ops:
  7.2 37.8 %copy-start.7 = (bf16[1536,48]{0,1:T(8,128)(2,1)S(1)}, bf16[1536,48]{0,1:T(8,128)(2,1)}, u32[]{:S(2)}) copy-start(bf16[1536,48]{0,1:T(8,128)(2,1)} %param.27) | copy-start | bytes 442372
  7.2 37.8 %copy-start.8 = (bf16[48,1536]{1,0:T(8,128)(2,1)S(1)}, bf16[48,1536]{1,0:T(8,128)(2,1)}, u32[]{:S(2)}) copy-start(bf16[48,1536]{1,0:T(8,128)(2,1)} %param.26) | copy-start | bytes 442372
  7.2 86.5 %all-gather.3.cloned.1.call-start = ((), (), s32[]{:S(2)}) async-start(), calls=%async_computation.1 | async-start | bytes 6082560 | tf_op jit(solution)/shard_map/all_gather | solution.py:1062
  9.7 164.2 %all-gather.5.cloned.1.call-start = ((), (), s32[]{:S(2)}) async-start(), calls=%async_computation.2 | async-start | bytes 9732096 | tf_op jit(solution)/shard_map/all_gather | solution.py:1062
  45.7 324.0 %reduce-scatter.2.cloned.1.call-start = ((), (), s32[]{:S(2)}) async-start(), calls=%async_computation.3 | async-start | bytes 9732096 | tf_op jit(solution)/shard_map/reduce_scatter | solution.py:1067
  47.1 10.6 %copy-start.12 = (s32[8,128]{1,0:T(8,128)S(1)}, s32[8,128]{1,0:T(8,128)}, u32[]{:S(2)}) copy-start(s32[8,128]{1,0:T(8,128)} %get-tuple-element.87) | copy-start | bytes 12292
  54.8 10.3 %collective-permute-start = (bf16[3,1024,384]{2,1,0:T(8,128)(2,1)}, bf16[3,1024,384]{2,1,0:T(8,128)(2,1)S(1)}, u32[]{:S(2)}, u32[]{:S(2)}) collective-permute-start(bf16[3,1024,384]{2,1,0:T(8,128)(2,1)} %get-tuple-element.85), channel_id=1, source_target_pairs={{0,2},{2,0},{1,3},{3,1},{4,6},{6,4},{5,7},{7,5},{8,10},{10,8},{9,1... | collective-permute-start | bytes 7077896 | tf_op jit(solution)/shard_map/ppermute | solution.py:1083
  55.8 37.9 %collective-permute-start.1 = (bf16[1500,768]{1,0:T(8,128)(2,1)}, bf16[1500,768]{1,0:T(8,128)(2,1)}, u32[]{:S(2)}, u32[]{:S(2)}) collective-permute-start(bf16[1500,768]{1,0:T(8,128)(2,1)} %bitcast.59), channel_id=1, source_target_pairs={{0,2},{2,0},{1,3},{3,1},{4,6},{6,4},{5,7},{7,5},{8,10},{10,8},{9,1... | collective-permute-start | bytes 6912008 | tf_op jit(solution)/shard_map/ppermute | solution.py:1083
  55.9 84.8 %collective-permute-start.3 = (bf16[1024,768]{1,0:T(8,128)(2,1)}, bf16[1024,768]{1,0:T(8,128)(2,1)}, u32[]{:S(2)}, u32[]{:S(2)}) collective-permute-start(bf16[1024,768]{1,0:T(8,128)(2,1)} %g_own_ref.1), channel_id=1, source_target_pairs={{1,2},{2,1},{5,6},{6,5},{9,10},{10,9},{13,14},{14,13},{17,18},{18,... | collective-permute-start | bytes 4718600 | tf_op jit(solution)/shard_map/ppermute | solution.py:1097
  65.1 1.4 copy-start.14
  66.5 26.6 %copy-start.13 = (f32[768]{0:T(1024)S(1)}, f32[768]{0:T(1024)}, u32[]{:S(2)}) copy-start(f32[768]{0:T(1024)} %param.32) | copy-start | bytes 9220
  92.6 10.3 %collective-permute-start.2 = (bf16[1024,384]{1,0:T(8,128)(2,1)}, bf16[1024,384]{1,0:T(8,128)(2,1)S(1)}, u32[]{:S(2)}, u32[]{:S(2)}) collective-permute-start(bf16[1024,384]{1,0:T(8,128)(2,1)} %get-tuple-element.91.o_sent_ref), channel_id=1, source_target_pairs={{0,2},{2,0},{1,3},{3,1},{4,6},{6,4},{5,7},{7,5},{8,10},{10,8},{9,1... | collective-permute-start | bytes 2359304 | tf_op jit(solution)/shard_map/ppermute | solution.py:1083
  102.9 0.9 copy-start.3
  225.9 1.4 copy-start.15
  227.3 123.0 %collective-permute-start.5 = (bf16[1024,768]{1,0:T(8,128)(2,1)S(1)}, bf16[1024,768]{1,0:T(8,128)(2,1)S(1)}, u32[]{:S(2)}, u32[]{:S(2)}) collective-permute-start(bf16[1024,768]{1,0:T(8,128)(2,1)S(1)} %copy-done.15), channel_id=1, source_target_pairs={{0,0},{1,2},{2,1},{3,3},{4,4},{5,6},{6,5},{7,7},{8,8},{9,10},{10,9... | collective-permute-start | bytes 4718600 | tf_op jit(solution)/shard_map/ppermute | solution.py:1082
  293.9 4.9 %collective-permute-start.4 = (bf16[1024,384]{1,0:T(8,128)(2,1)}, bf16[1024,384]{1,0:T(8,128)(2,1)S(1)}, u32[]{:S(2)}, u32[]{:S(2)}) collective-permute-start(bf16[1024,384]{1,0:T(8,128)(2,1)} %get-tuple-element.109), channel_id=1, source_target_pairs={{0,2},{2,0},{1,3},{3,1},{4,6},{6,4},{5,7},{7,5},{8,10},{10,8},{9,1... | collective-permute-start | bytes 2359304 | tf_op jit(solution)/shard_map/ppermute | solution.py:1083
  298.9 0.9 copy-start.16
  350.3 1.1 copy-start.1
  351.5 18.2 %collective-permute-start.6 = (bf16[3,1024,384]{2,1,0:T(8,128)(2,1)}, bf16[3,1024,384]{2,1,0:T(8,128)(2,1)S(1)}, u32[]{:S(2)}, u32[]{:S(2)}) collective-permute-start(bf16[3,1024,384]{2,1,0:T(8,128)(2,1)} %get-tuple-element.124), channel_id=1, source_target_pairs={{0,2},{2,0},{1,3},{3,1},{4,6},{6,4},{5,7},{7,5},{8,10},{10,8},{9,1... | collective-permute-start | bytes 7077896 | tf_op jit(solution)/shard_map/ppermute | solution.py:1083
  369.7 1.4 copy-start
  458.1 3.5 copy-start.2
  461.5 1.2 copy-start.6
  461.5 1.9 copy-start.11
  461.5 2.5 copy-start.10
  461.5 3.1 copy-start.9
  461.5 3.8 copy-start.5
  461.5 4.5 copy-start.4
Sparse Core Ops, SparseCore 0:
  11.5 78.2 all-gather.2
  93.2 80.6 all-gather.4
  226.0 134.1 reduce-scatter.1

commit v2 on v1

--- a/solution.py
+++ b/solution.py
@@ -276,7 +276,6 @@
 
 EPSILON = 1e-05
 ROWS = 256
-CHUNK = 768
 BIG = 60 * 2**20
 
 
@@ -429,7 +428,7 @@
     return phi, phi + v * bell * 0.3989422804014327
 
 
-def feed_kernel(mine_ref, attn_ref, resid_ref, g_own_ref, g_come_ref, wo_ref, wi_ref, wm_ref, gain_ref, shift_ref, bias_ref, unit_bias_ref, out_bias_ref,
+def feed_kernel(mine_ref, attn_ref, resid_ref, g_own_ref, g_come_ref, wo_ref, wi_ref, wm_low_ref, wm_high_ref, gain_ref, shift_ref, bias_ref, unit_bias_ref, out_bias_ref,
                 out_ref, norm_ref, hidden_ref, dpre_ref, g2_ref, dattn_ref, g_ref,
                 sum_g_ref, sum_dpre_ref, sum_g2_ref, sum_gain_ref, sum_shift_ref):
     part = wo_ref.shape[2]
@@ -445,28 +444,30 @@
     out = resid + out_bias_ref[...]
     back = jnp.zeros_like(resid)
     sums = []
-    spots = [(t, c) for t in range(2) for c in range(0, units, CHUNK)]
+    chunk = units // 2
+    spots = [(t, c) for t in range(2) for c in (0, chunk)]
+    wm = {0: wm_low_ref, chunk: wm_high_ref}
 
     def first(spot):
         t, c = spot
-        at = slice(t * units + c, t * units + c + CHUNK)
-        return nn(low, wi_ref[t, :, c:c + CHUNK]) + unit_bias_ref[:, at], nn(g_low, wm_ref[t, :, c:c + CHUNK])
+        at = slice(t * units + c, t * units + c + chunk)
+        return nn(low, wi_ref[t, :, c:c + chunk]) + unit_bias_ref[:, at], nn(g_low, wm[c][t])
 
     ahead = first(spots[0])
     for k, (t, c) in enumerate(spots):
-        at = slice(t * units + c, t * units + c + CHUNK)
+        at = slice(t * units + c, t * units + c + chunk)
         pre, back_hidden = ahead
         if k + 1 < len(spots):
             ahead = first(spots[k + 1])
         phi, slope = gelu_parts(pre)
         hidden = (pre * phi).astype(BF)
         hidden_ref[:, at] = hidden
-        out = out + nt(hidden, wm_ref[t, :, c:c + CHUNK])
+        out = out + nt(hidden, wm[c][t])
         dpre = back_hidden * slope
         sums.append(column_sum(dpre))
         dpre = dpre.astype(BF)
         dpre_ref[:, at] = dpre
-        back = back + nt(dpre, wi_ref[t, :, c:c + CHUNK])
+        back = back + nt(dpre, wi_ref[t, :, c:c + chunk])
     out_ref[...] = out.astype(BF)
     sums = jnp.concatenate(sums, 1)
     wide = sum_dpre_ref.shape[1]
@@ -483,16 +484,16 @@
         dattn_ref[:, t * part:(t + 1) * part] = nn(g2_low, wo_ref[t]).astype(BF)
 
 
-def feed(mine, attn, resid, g_own, g_come, w_mid, w_ff, gain, shift, bias, unit_bias, out_bias):
+def feed(mine, attn, resid, g_own, g_come, w_mid, w_ff, w_high, gain, shift, bias, unit_bias, out_bias):
     rows, width = resid.shape
     part = width // 2
-    units = w_ff.shape[2] // 2
+    units = 2 * w_high.shape[2]
     w_at = lambda cols, c: pl.BlockSpec((2, width, cols), lambda i: (0, 0, c), pipeline_mode=pl.Buffered(1))
     line = lambda count: (pl.BlockSpec((count, width), lambda i: (0, 0)), shaped((count, width), F32))
     lines = [line(1), line(2 * units // width), line(1), line(1), line(1)]
     return pl.pallas_call(
         feed_kernel, grid=(rows // ROWS,),
-        in_specs=[scalar(), by_rows(width), by_rows(width), by_rows(width), by_rows(width), w_at(part, 4), w_at(units, 0), w_at(units, 1),
+        in_specs=[scalar(), by_rows(width), by_rows(width), by_rows(width), by_rows(width), w_at(part, 4), w_at(units, 0), w_at(units // 2, 2), whole(w_high.shape),
                   whole(gain.shape), whole(shift.shape), whole(bias.shape), whole(unit_bias.shape), whole(out_bias.shape)],
         out_specs=[by_rows(width), by_rows(width), by_rows(2 * units), by_rows(2 * units), by_rows(width), by_rows(width), by_rows(width)] + [a for a, _ in lines],
         out_shape=[shaped((rows, width), BF), shaped((rows, width), BF), shaped((rows, 2 * units), BF), shaped((rows, 2 * units), BF),
@@ -500,7 +501,7 @@
         compiler_params=pltpu.CompilerParams(vmem_limit_bytes=BIG),
         cost_estimate=cost(2 * rows * width * (2 * width + 8 * units), 2 * width * (width + 4 * units) + 2 * rows * (8 * width + 4 * units), 4 * rows * units),
         name="feed",
-    )(mine, attn, resid, g_own, g_come, w_mid, w_ff, w_ff, gain, shift, bias, unit_bias, out_bias)
+    )(mine, attn, resid, g_own, g_come, w_mid, w_ff, w_ff, w_high, gain, shift, bias, unit_bias, out_bias)
 
 
 def feed_weights_kernel(norm_ref, g_ref, dpre_ref, hidden_ref, out_ref):
@@ -705,20 +706,24 @@
                 copy.wait()
 
 
-def gather_kernel(names, orders, own_ref, seg_ref, x_ref, out_ref, seg_out_ref, moved_ref, block, segs, local_sem, send_sem, recv_sem,
+def gather_kernel(names, orders, own_ref, more_ref, seg_ref, x_ref, out_ref, more_out_ref, seg_out_ref, moved_ref, block, segs, local_sem, send_sem, recv_sem,
                   swap_send, swap_recv):
     core, tensor = lax.axis_index("core"), lax.axis_index("tensor")
     greet(names, {"core": 1 - core, "tensor": 1 - tensor})
-    spare = len(orders)
+    spare = 2 * len(orders)
     swap = Swap(x_ref, moved_ref, swap_send, swap_recv)
     pieces, _, part = own_ref.shape
     for i in range(pieces):
         block[:, i * part:(i + 1) * part] = own_ref[i]
-    lanes = stream_cols(block.shape[1], len(orders))
+    cut = more_ref.shape[1] - more_out_ref.shape[-1]
+    more = more_ref.at[:, cut:]
+    streams = [(order, block.at[:, lane], out_ref, lane) for order, lane in zip(orders, stream_cols(block.shape[1], len(orders)))]
+    streams += [(order, more_ref.at[:, cut + lane.start:cut + lane.stop], more_out_ref, lane)
+                for order, lane in zip(orders, stream_cols(more_out_ref.shape[-1], len(orders)))]
     place = tuple(my_bit(n) for n in names)
-    known = [[] for _ in orders]
+    known = [[] for _ in streams]
     sent = []
-    flying = [None] * len(orders)
+    flying = [None] * len(streams)
 
     def send(src, dst, st, step, name):
         copy = pltpu.make_async_remote_copy(src, dst, send_sem.at[st, step], recv_sem.at[st, step],
@@ -728,22 +733,26 @@
         return copy
 
     def start(st, step):
-        name = orders[st][step]
+        order, own, full, lane = streams[st]
+        name = order[step]
         at = tuple(slice(None) if n in known[st] else my_bit(n) for n in names)
-        dst = out_ref.at[at + (slice(None), lanes[st])]
-        flying[st] = send(dst if step else block.at[:, lanes[st]], dst, st, step, name)
+        dst = full.at[at + (slice(None), lane)]
+        flying[st] = send(dst if step else own, dst, st, step, name)
         known[st].append(name)
 
-    for st in range(len(orders)):
+    for st in range(len(streams)):
         start(st, 0)
     local = pltpu.make_async_copy(block, out_ref.at[place], local_sem.at[0])
     local.start()
+    local_more = pltpu.make_async_copy(more, more_out_ref.at[place], local_sem.at[1])
+    local_more.start()
     segs[core, tensor] = seg_ref[...]
     along = send(segs.at[core, tensor], segs.at[core, tensor], spare, 0, "t")
     swap.some(2)
     local.wait()
+    local_more.wait()
     for step in range(len(names)):
-        for st in range(len(orders)):
+        for st in range(len(streams)):
             flying[st].wait_recv()
             if step + 1 < len(names):
                 start(st, step + 1)
@@ -758,7 +767,7 @@
     swap.wait()
 
 
-def gather_all(shard, seg, x, chips):
+def gather_all(shard, more, more_cols, seg, x, chips):
     names = bit_names(chips)
     orders = [list(reversed(o)) for o in exchange_orders(names)]
     pieces, rows, part = shard.shape
@@ -767,17 +776,18 @@
     vmem = pl.BlockSpec(memory_space=pltpu.VMEM)
     seg = seg.reshape(-1, LANES)
     hbm = pl.BlockSpec(memory_space=pl.ANY)
-    full, seg, moved = pl.pallas_call(
+    full, more, seg, moved = pl.pallas_call(
         functools.partial(gather_kernel, names, orders),
-        in_specs=[vmem, vmem, hbm], out_specs=[hbm, vmem, hbm],
-        out_shape=[shaped((2,) * len(names) + (rows, cols), shard.dtype), shaped(seg.shape, seg.dtype), shaped(x.shape, x.dtype)],
+        in_specs=[vmem, vmem, vmem, hbm], out_specs=[hbm, hbm, vmem, hbm],
+        out_shape=[shaped((2,) * len(names) + (rows, cols), shard.dtype),
+                   shaped((2,) * len(names) + (rows, more_cols), shard.dtype), shaped(seg.shape, seg.dtype), shaped(x.shape, x.dtype)],
         scratch_shapes=[pltpu.VMEM((rows, cols), shard.dtype), pltpu.VMEM((2, 2) + seg.shape, seg.dtype),
-                        dma((2,)), dma((len(orders) + 1, len(names))), dma((len(orders) + 1, len(names))),
+                        dma((2,)), dma((2 * len(orders) + 1, len(names))), dma((2 * len(orders) + 1, len(names))),
                         dma((CHUNKS,)), dma((CHUNKS,))],
         compiler_params=pltpu.CompilerParams(collective_id=0, has_side_effects=True, vmem_limit_bytes=BIG),
         cost_estimate=cost(0, 1e6), name="gather_all",
-    )(shard, seg, x)
-    return full.reshape(2, -1, cols), seg.reshape(-1), moved
+    )(shard, more, seg, x)
+    return full.reshape(2, -1, cols), more.reshape(2, -1, more_cols), seg.reshape(-1), moved
 
 
 class Sums:
@@ -1086,9 +1096,9 @@
     mid = jnp.concatenate([attn_out.T, cross_q, cross_kv.reshape(rows_here, 2 * part), cross_out.T], 1)
     first, mid = lax.optimization_barrier((attn_in.transpose(1, 0, 2), mid))
     w_mid = fetch(mid)
-    w_qkv, seg_cont, x_come = gather_all(first, seg_ids, tokens, chips)
+    w_qkv, w_high, seg_cont, x_come = gather_all(first, mlp_out.T, units // 2, seg_ids, tokens, chips)
     late_in, late_out, w_qkv = lax.optimization_barrier((mlp_in, mlp_out, w_qkv))
-    w_ff = fetch(jnp.concatenate([late_in, late_out.T], 1))
+    w_ff = fetch(jnp.concatenate([late_in, late_out.T[:, :units // 2]], 1))
     bias_halves = proj_bias[:2].reshape(2, 2, part).transpose(1, 0, 2)
 
     norm_one, sent, moved = qkv_sent(core_at, mine, tokens, x_come, w_qkv, norm_gain, norm_bias, bias_halves)
@@ -1103,7 +1113,7 @@
     resid_one, norm_two, q_cross = middle(core_at, moved, o_kept, o_come, w_mid, norm_gain, norm_bias, proj_bias)
     attn_cross, lse_cross = cross_fwd(q_cross, kv, frames, heads)
     (out, norm_three, hidden, dpre, g_two, dattn, grad_in, sum_g, sum_dpre, sum_g_two, gain_three, shift_three) = feed(
-        mine, attn_cross, resid_one, grad_output, grad_come, w_mid, w_ff, norm_gain, norm_bias, proj_bias, mlp_bias[None], out_bias[None])
+        mine, attn_cross, resid_one, grad_output, grad_come, w_mid, w_ff, w_high, norm_gain, norm_bias, proj_bias, mlp_bias[None], out_bias[None])
     output = fix(out)
     gw_ff = feed_weights(norm_three, grad_in, dpre, hidden)
     dattn, gw_ff = lax.optimization_barrier((dattn, gw_ff))

time: 483 us -> 467 us (0.967); the launches traced: 473 us -> 464 us
  waiting for transfers between devices: 35.4 us -> 13.1 us
  Pallas kernels: 387 us -> 399 us
    all_gather x2, waiting for transfers between devices: 33.2 us -> 10.9 us  [fetch(): full = lax.all_gather(shard, ALL, axis=0, tiled=True)]
    pallas_call x1, Pallas kernels: 35.2 us -> 48.2 us  [gather_all(): pl.pallas_call(functools.partial(gather_kernel, names, orders), in_specs=...]
  transfers between devices with their start and end apart: 10 -> 10, of which waited for: 2 -> 2; matrix products, arithmetic and copies ran while one was open for 1% -> 1% of each run, Pallas kernels for 54% -> 58%
where the time goes in v2:
time: 467 us; the launch traced here: 464 us
  Pallas kernels  399 us (85%)
  local copies, waits for them, and re-layouts  22.5 us (5%)
  between operations  14.2 us (3%)
  waiting for transfers between devices  13.1 us (3%)
  starting transfers between devices  8.27 us (2%)
  other arithmetic  6.55 us (1%)
    pallas_call x1, Pallas kernels, end_all(): pl.pallas_call(functools.partial(end_kernel, names, orders, mid_lanes, qk...  78.8 us
    pallas_call x1, Pallas kernels, cross_bwd(): pl.pallas_call(functools.partial(cross_bwd_kernel, frames), grid=(npair,)...  56.1 us
    pallas_call x1, Pallas kernels, self_bwd(): pl.pallas_call(self_bwd_kernel, grid=(part // LANES,), in_specs=[scalar()...  50.4 us
    pallas_call x1, Pallas kernels, gather_all(): pl.pallas_call(functools.partial(gather_kernel, names, orders), in_specs=...  48.2 us
    pallas_call x1, Pallas kernels, feed(): pl.pallas_call(feed_kernel, grid=(rows // ROWS,), in_specs=[scalar(), by_...  36.5 us
    pallas_call x1, Pallas kernels, cross_fwd(): pl.pallas_call(functools.partial(cross_fwd_kernel, frames), grid=(npair,)...  27.5 us
    pallas_call x1, Pallas kernels, self_fwd(): pl.pallas_call(self_fwd_kernel, grid=(part // LANES,), in_specs=[scalar()...  26.1 us
    pallas_call x1, Pallas kernels, middle_weights(): pl.pallas_call(middle_weights_kernel, grid=(2,), in_specs=[scalar(), whol...  17.8 us
  transfers between devices with their start and end apart: 10, of which 2 were waited for; matrix products, arithmetic and copies ran while one was open for 1% of the time, Pallas kernels for 58%

profile of v2, /device:TPU:0, one launch (start us, length us, event | category | flops | bytes accessed | tf_op | source)
XLA Modules:
  0.0 464.1 jit_solution(16564089494583719663)
XLA Ops:
  7.2 1.0 copy.34
  8.2 1.5 pad_maximum_fusion.1
  9.8 48.2 %gather_all.1 = (bf16[2,2,2,2,2,48,1152]{6,5,4,3,2,1,0:T(8,128)(2,1)}, bf16[2,2,2,2,2,48,768]{6,5,4,3,2,1,0:T(8,128)(2,1)}, s32[8,128]{1,0:T(8,128)}, bf16[1024,768]{1,0:T(8,128)(2,1)}) custom-call(bf16[3,48,384]{2,1,0:T(8,128)(2,1)} %bitcast.46, bf16[48,1536]{1,0:T(8,128)(2,1)} %bitcast.41, s32[8,128]{1,0:T(8,128)} %bitcast.56, bf16[1024,768]{1,0:T(8,128)(2,1)} %x_own_ref.1), custom_call_target="tpu_custom_call" | custom-call | bytes 1000000 | tf_op jit(solution)/shard_map/gather_all/pallas_call | solution.py:779
  58.8 1.3 slice.21
  60.2 7.7 %qkv_sent.1 = (bf16[1024,768]{1,0:T(8,128)(2,1)}, bf16[3,1024,384]{2,1,0:T(8,128)(2,1)}, bf16[1024,768]{1,0:T(8,128)(2,1)}) custom-call(s32[1]{0:T(128)} %bitcast.core_ref, s32[1]{0:T(128)} %bitcast.1.mine_ref, bf16[1024,768]{1,0:T(8,128)(2,1)} %x_own_ref.1, bf16[1024,768]{1,0:T(8,128)(2,1)} %get-tuple-element.82.x_come_ref, bf16[2,768,1152]{2,1,0:T(8,128)(2,1)} %bitcast.36, ...), custom_call_target="tpu_custom_call" | custom-call | flops 1811939328 | bytes 9830400 | tf_op jit(solution)/shard_map/qkv_sent/pallas_call | solution.py:343
  68.4 2.0 collective-permute-start.3
  70.4 1.0 copy.31.segq_ref.segk_ref
  71.5 6.3 %qkv_kept.1.kept_ref = bf16[3,1024,384]{2,1,0:T(8,128)(2,1)} custom-call(s32[1]{0:T(128)} %bitcast.core_ref, bf16[1024,768]{1,0:T(8,128)(2,1)} %get-tuple-element.85.norm_ref.norm_hbm, bf16[2,768,1152]{2,1,0:T(8,128)(2,1)} %bitcast.37, f32[2,2,384]{2,1,0:T(2,128)} %bitcast.53), custom_call_target="tpu_custom_call" | custom-call | flops 1811939328 | bytes 8257536 | tf_op jit(solution)/shard_map/qkv_kept/pallas_call | solution.py:356
  77.7 1.4 copy-done.14
  79.1 26.1 %self_fwd.1 = (bf16[1024,384]{1,0:T(8,128)(2,1)}, bf16[1024,384]{1,0:T(8,128)(2,1)}, f32[2048,384]{1,0:T(8,128)}) custom-call(s32[1]{0:T(128)} %bitcast.core_ref, bf16[3,1024,384]{2,1,0:T(8,128)(2,1)} %qkv_kept.1.kept_ref, bf16[3,1024,384]{2,1,0:T(8,128)(2,1)} %copy-done.14, s32[1024,1]{1,0:T(8,128)} %copy.31.segq_ref.segk_ref, s32[1,1024]{1,0:T(1,128)} %bitcast.57), custom_call_target="tpu_custom_call" | custom-call | flops 1811939328 | bytes 1179648 | tf_op jit(solution)/shard_map/self_fwd/pallas_call | solution.py:86
  105.3 1.6 collective-permute-start.2
  107.5 9.2 %memory_project.1 = (bf16[1536,1536]{1,0:T(8,128)(2,1)}, bf16[1536,768]{1,0:T(8,128)(2,1)}) custom-call(s32[1]{0:T(128)} %bitcast.1.mine_ref, bf16[1500,768]{1,0:T(8,128)(2,1)} %bitcast.64, bf16[1500,768]{1,0:T(8,128)(2,1)} %collective-permute-done.1.come_ref, bf16[2,768,1920]{2,1,0:T(8,128)(2,1)} %bitcast.30, f32[6,768]{1,0:T(8,128)} %bias_ref.5), custom_call_target="tpu_custom_call" | custom-call | flops 3538944000 | bytes 13879296 | tf_op jit(solution)/shard_map/memory_project/pallas_call | solution.py:381
  117.6 9.5 %middle.1 = (f32[1024,768]{1,0:T(8,128)}, bf16[1024,768]{1,0:T(8,128)(2,1)}, bf16[1024,768]{1,0:T(8,128)(2,1)}) custom-call(s32[1]{0:T(128)} %bitcast.core_ref, bf16[1024,768]{1,0:T(8,128)(2,1)} %get-tuple-element.87.x_ref.x_hbm, bf16[1024,384]{1,0:T(8,128)(2,1)} %get-tuple-element.89.own_ref.o_ref, bf16[1024,384]{1,0:T(8,128)(2,1)} %copy-done.3, ...), custom_call_target="tpu_custom_call" | custom-call | flops 2415919104 | bytes 11796480 | tf_op jit(solution)/shard_map/middle/pallas_call | solution.py:410
  127.1 27.5 %cross_fwd.1 = (bf16[1024,768]{1,0:T(8,128)(2,1)}, f32[1024,768]{1,0:T(8,128)}) custom-call(bf16[1024,768]{1,0:T(8,128)(2,1)} %get-tuple-element.94.q_ref, bf16[1536,1536]{1,0:T(8,128)(2,1)} %get-tuple-element.95.k_ref.v_ref, bf16[1536,1536]{1,0:T(8,128)(2,1)} %get-tuple-element.95.k_ref.v_ref), custom_call_target="tpu_custom_call" | custom-call | flops 2415919104 | bytes 1376256 | tf_op jit(solution)/shard_map/cross_fwd/pallas_call | solution.py:129
  154.5 10.9 %all-gather.5.cloned.1.call-done = bf16[1536,2304]{1,0:T(8,128)(2,1)} async-done(((bf16[48,2304]{1,0:T(8,128)(2,1)}), bf16[1536,2304]{1,0:T(8,128)(2,1)}) %all-gather.5.cloned.1.call-update) | async-done | bytes 7077904 | tf_op jit(solution)/shard_map/all_gather | solution.py:1072
  165.4 36.5 %feed.1 = (bf16[1024,768]{1,0:T(8,128)(2,1)}, bf16[1024,768]{1,0:T(8,128)(2,1)}, bf16[1024,3072]{1,0:T(8,128)(2,1)}, bf16[1024,3072]{1,0:T(8,128)(2,1)}, f32[102...) custom-call(s32[1]{0:T(128)} %bitcast.1.mine_ref, ...), custom_call_target="tpu_custom_call" | custom-call | flops 21743271936 | bytes 35782656 | tf_op jit(solution)/shard_map/feed/pallas_call | solution.py:494
  201.9 15.6 %feed_weights.1 = bf16[2,768,3072]{2,1,0:T(8,128)(2,1)} custom-call(bf16[1024,768]{1,0:T(8,128)(2,1)} %get-tuple-element.102.norm_ref, bf16[1024,768]{1,0:T(8,128)(2,1)} %get-tuple-element.103.g_ref, bf16[1024,3072]{1,0:T(8,128)(2,1)} %get-tuple-element.104.dpre_ref, bf16[1024,3072]{1,0:T(8,128)(2,1)} %get-tuple-element.105.hidden_ref), custom_call_target="tpu_custom_call" | custom-call | flops 9663676416 | bytes 22020096 | tf_op jit(solution)/shard_map/feed_weights/pallas_call | solution.py:517
  217.5 1.4 copy-done.15
  219.7 56.1 %cross_bwd.1 = (bf16[1024,768]{1,0:T(8,128)(2,1)}, bf16[1536,768]{1,0:T(8,128)(2,1)}, bf16[1536,768]{1,0:T(8,128)(2,1)}) custom-call(bf16[1024,768]{1,0:T(8,128)(2,1)} %get-tuple-element.94.q_ref, bf16[1536,1536]{1,0:T(8,128)(2,1)} %get-tuple-element.95.k_ref.v_ref, bf16[1536,1536]{1,0:T(8,128)(2,1)} %get-tuple-element.95.k_ref.v_ref, ...), custom_call_target="tpu_custom_call" | custom-call | flops 6039797760 | bytes 2359296 | tf_op jit(solution)/shard_map/cross_bwd/pallas_call | solution.py:263
  275.7 9.8 %middle_back.1 = (f32[1024,768]{1,0:T(8,128)}, bf16[1024,384]{1,0:T(8,128)(2,1)}, bf16[1024,384]{1,0:T(8,128)(2,1)}, f32[1,768]{1,0:T(1,128)}, f32[1,768]{1,0:T(...) custom-call(s32[1]{0:T(128)} %bitcast.core_ref, bf16[1024,768]{1,0:T(8,128)(2,1)} %get-tuple-element.120.dq_ref, ...), custom_call_target="tpu_custom_call" | custom-call | flops 2415919104 | bytes 16515072 | tf_op jit(solution)/shard_map/middle_back/pallas_call | solution.py:551
  285.6 2.8 collective-permute-start.4
  288.4 2.1 collective-permute-done.4.do_come_ref
  291.4 50.4 %self_bwd.1 = (bf16[3,1024,384]{2,1,0:T(8,128)(2,1)}, bf16[3,1024,384]{2,1,0:T(8,128)(2,1)}) custom-call(s32[1]{0:T(128)} %bitcast.core_ref, bf16[3,1024,384]{2,1,0:T(8,128)(2,1)} %qkv_kept.1.kept_ref, bf16[3,1024,384]{2,1,0:T(8,128)(2,1)} %copy-done.14, bf16[1024,384]{1,0:T(8,128)(2,1)} %get-tuple-element.110.do_ref, bf16[1024,384]{1,0:T(8,128)(2,1)} %copy-done.16, ...), custom_call_target="tpu_custom_call" | custom-call | flops 4529848320 | bytes 1966080 | tf_op jit(solution)/shard_map/self_bwd/pallas_call | solution.py:226
  341.8 1.1 copy-done.1
  343.4 17.8 %middle_weights.1 = (bf16[2,768,1920]{2,1,0:T(8,128)(2,1)}, f32[1,768]{1,0:T(1,128)}) custom-call(s32[1]{0:T(128)} %bitcast.core_ref, f32[1024,768]{1,0:T(8,128)} %get-tuple-element.117.g1_ref.g1_hbm, bf16[1024,384]{1,0:T(8,128)(2,1)} %get-tuple-element.89.own_ref.o_ref, bf16[1024,384]{1,0:T(8,128)(2,1)} %copy-done.3, ...), custom_call_target="tpu_custom_call" | custom-call | flops 7247757312 | bytes 28704768 | tf_op jit(solution)/shard_map/middle_weights/pallas_call | solution.py:579
  361.2 1.4 copy-done
  362.6 78.8 %end_all.1 = (f32[3,48,384]{2,1,0:T(8,128)}, f32[48,384]{1,0:T(8,128)}, f32[48,384]{1,0:T(8,128)}, f32[48,384]{1,0:T(8,128)}, f32[48,384]{1,0:T(8,128)}, /*index...) custom-call(bf16[2,2,2,2,2,48,1920]{6,5,4,3,2,1,0:T(8,128)(2,1)} %bi, ...), custom_call_target="tpu_custom_call" | custom-call | bytes 1000000 | tf_op jit(solution)/shard_map/end_all/pallas_call | solution.py:1054
  441.4 1.3 slice_reduce_fusion
  443.5 1.4 slice.25
  444.9 1.4 fusion
  448.6 3.4 convert_element_type.4
  452.1 1.1 copy.42
  (61 shorter events, 12.1 us)
Async XLA Ops:
  7.2 50.8 %copy-start.4 = (bf16[1536,48]{0,1:T(8,128)(2,1)S(1)}, bf16[1536,48]{0,1:T(8,128)(2,1)}, u32[]{:S(2)}) copy-start(bf16[1536,48]{0,1:T(8,128)(2,1)} %param.27) | copy-start | bytes 442372
  7.2 50.8 %copy-start.8 = (bf16[48,1536]{1,0:T(8,128)(2,1)S(1)}, bf16[48,1536]{1,0:T(8,128)(2,1)}, u32[]{:S(2)}) copy-start(bf16[48,1536]{1,0:T(8,128)(2,1)} %param.26) | copy-start | bytes 442372
  7.2 100.3 %all-gather.3.cloned.1.call-start = ((), (), s32[]{:S(2)}) async-start(), calls=%async_computation.1 | async-start | bytes 6082560 | tf_op jit(solution)/shard_map/all_gather | solution.py:1072
  9.7 155.7 %all-gather.5.cloned.1.call-start = ((), (), s32[]{:S(2)}) async-start(), calls=%async_computation.2 | async-start | bytes 7299072 | tf_op jit(solution)/shard_map/all_gather | solution.py:1072
  58.8 302.4 %reduce-scatter.2.cloned.1.call-start = ((), (), s32[]{:S(2)}) async-start(), calls=%async_computation.3 | async-start | bytes 9732096 | tf_op jit(solution)/shard_map/reduce_scatter | solution.py:1077
  60.2 10.3 %copy-start.12 = (s32[8,128]{1,0:T(8,128)S(1)}, s32[8,128]{1,0:T(8,128)}, u32[]{:S(2)}) copy-start(s32[8,128]{1,0:T(8,128)} %get-tuple-element.88) | copy-start | bytes 12292
  67.9 9.9 %collective-permute-start = (bf16[3,1024,384]{2,1,0:T(8,128)(2,1)}, bf16[3,1024,384]{2,1,0:T(8,128)(2,1)S(1)}, u32[]{:S(2)}, u32[]{:S(2)}) collective-permute-start(bf16[3,1024,384]{2,1,0:T(8,128)(2,1)} %get-tuple-element.86), channel_id=1, source_target_pairs={{0,2},{2,0},{1,3},{3,1},{4,6},{6,4},{5,7},{7,5},{8,10},{10,8},{9,1... | collective-permute-start | bytes 7077896 | tf_op jit(solution)/shard_map/ppermute | solution.py:1093
  68.3 39.2 %collective-permute-start.1 = (bf16[1500,768]{1,0:T(8,128)(2,1)}, bf16[1500,768]{1,0:T(8,128)(2,1)}, u32[]{:S(2)}, u32[]{:S(2)}) collective-permute-start(bf16[1500,768]{1,0:T(8,128)(2,1)} %bitcast.63), channel_id=1, source_target_pairs={{0,2},{2,0},{1,3},{3,1},{4,6},{6,4},{5,7},{7,5},{8,10},{10,8},{9,1... | collective-permute-start | bytes 6912008 | tf_op jit(solution)/shard_map/ppermute | solution.py:1093
  68.4 86.1 %collective-permute-start.3 = (bf16[1024,768]{1,0:T(8,128)(2,1)}, bf16[1024,768]{1,0:T(8,128)(2,1)}, u32[]{:S(2)}, u32[]{:S(2)}) collective-permute-start(bf16[1024,768]{1,0:T(8,128)(2,1)} %g_own_ref.1), channel_id=1, source_target_pairs={{1,2},{2,1},{5,6},{6,5},{9,10},{10,9},{13,14},{14,13},{17,18},{18,... | collective-permute-start | bytes 4718600 | tf_op jit(solution)/shard_map/ppermute | solution.py:1107
  77.7 1.4 copy-start.14
  79.1 27.7 %copy-start.13 = (f32[768]{0:T(1024)S(1)}, f32[768]{0:T(1024)}, u32[]{:S(2)}) copy-start(f32[768]{0:T(1024)} %param.32) | copy-start | bytes 9220
  105.3 11.4 %collective-permute-start.2 = (bf16[1024,384]{1,0:T(8,128)(2,1)}, bf16[1024,384]{1,0:T(8,128)(2,1)S(1)}, u32[]{:S(2)}, u32[]{:S(2)}) collective-permute-start(bf16[1024,384]{1,0:T(8,128)(2,1)} %get-tuple-element.92.o_sent_ref), channel_id=1, source_target_pairs={{0,2},{2,0},{1,3},{3,1},{4,6},{6,4},{5,7},{7,5},{8,10},{10,8},{9,1... | collective-permute-start | bytes 2359304 | tf_op jit(solution)/shard_map/ppermute | solution.py:1093
  116.6 0.9 copy-start.3
  217.5 1.4 copy-start.15
  218.9 122.9 %collective-permute-start.5 = (bf16[1024,768]{1,0:T(8,128)(2,1)S(1)}, bf16[1024,768]{1,0:T(8,128)(2,1)S(1)}, u32[]{:S(2)}, u32[]{:S(2)}) collective-permute-start(bf16[1024,768]{1,0:T(8,128)(2,1)S(1)} %copy-done.15), channel_id=1, source_target_pairs={{0,0},{1,2},{2,1},{3,3},{4,4},{5,6},{6,5},{7,7},{8,8},{9,10},{10,9... | collective-permute-start | bytes 4718600 | tf_op jit(solution)/shard_map/ppermute | solution.py:1092
  285.6 4.9 %collective-permute-start.4 = (bf16[1024,384]{1,0:T(8,128)(2,1)}, bf16[1024,384]{1,0:T(8,128)(2,1)S(1)}, u32[]{:S(2)}, u32[]{:S(2)}) collective-permute-start(bf16[1024,384]{1,0:T(8,128)(2,1)} %get-tuple-element.111), channel_id=1, source_target_pairs={{0,2},{2,0},{1,3},{3,1},{4,6},{6,4},{5,7},{7,5},{8,10},{10,8},{9,1... | collective-permute-start | bytes 2359304 | tf_op jit(solution)/shard_map/ppermute | solution.py:1093
  290.5 0.9 copy-start.16
  341.8 1.1 copy-start.1
  342.9 18.2 %collective-permute-start.6 = (bf16[3,1024,384]{2,1,0:T(8,128)(2,1)}, bf16[3,1024,384]{2,1,0:T(8,128)(2,1)S(1)}, u32[]{:S(2)}, u32[]{:S(2)}) collective-permute-start(bf16[3,1024,384]{2,1,0:T(8,128)(2,1)} %get-tuple-element.126), channel_id=1, source_target_pairs={{0,2},{2,0},{1,3},{3,1},{4,6},{6,4},{5,7},{7,5},{8,10},{10,8},{9,1... | collective-permute-start | bytes 7077896 | tf_op jit(solution)/shard_map/ppermute | solution.py:1093
  361.2 1.4 copy-start
  448.6 3.5 copy-start.2
  452.1 1.2 copy-start.7
  452.1 1.9 copy-start.11
  452.1 2.5 copy-start.10
  452.1 3.1 copy-start.9
  452.1 3.8 copy-start.6
  452.1 4.5 copy-start.5
Sparse Core Ops, SparseCore 0:
  11.5 78.3 all-gather.2
  93.3 72.0 all-gather.4
  217.6 134.1 reduce-scatter.1
